TPU v7x, 256 devices: a whole 4x4x8 slice. The times are simulated.
256 devices in a mesh: section: 4 (over z_hi, core), kv: 16 (over z_lo, y), tp: 4 (over x).
Axes of the slice: x: 4, y: 4, z: 8 (z_hi: 2, z_lo: 4; z = z_hi * 4 + z_lo), core: 2. Of those that a mesh axis runs over, the one named last changes fastest.
Arguments:
- patches: bfloat16 [32768, 1152], P(('section', 'kv'), 'tp'), may hold values from -6 to 6
- vis_gain: float32 [1152], replicated, may hold values from 0.1 to 1.9
- vis_bias: float32 [1152], replicated, may hold values from -3 to 3
- w_proj: bfloat16 [1152, 4608], P('section', 'tp')
- b_proj: float32 [4608], P('tp'), may hold values from -12 to 12
- rms_gain: float32 [4608], P('tp'), may hold values from 0.1 to 1.9
- w_kv: bfloat16 [4608, 2, 1024], P('tp'), may hold values from -0.09375 to 0.09375
- queries: bfloat16 [16, 2048], P('section', 'tp'), may hold values from -18 to 18
- cache: bfloat16 [1024, 128, 2, 1024], P(('section', 'kv'), None, None, 'tp'), may hold values from -6 to 6
- cache_lengths: int32 [4, 4], P('section'), may hold values from 1 to 31872, 32256 in all within a row
- slot_page: int32 [4, 256], P('section', 'kv'), may hold values from 0 to 255, each once within a row
- page_owner: int32 [4, 64], replicated, may hold values from 0 to 15, as said below
- image_request: int32 [4, 2], P('section'), may hold values from 0 to 3
Outputs:
- new_pages: bfloat16 [2048, 128, 2, 1024], P(('section', 'kv'), None, None, 'tp')
- attended: bfloat16 [16, 2048], P('section', 'tp')
Inputs may be any that keep to these rules, and one draw needn't show every extreme that they name: `page_owner`: from each source's 4 pages at most 2 go to any one owner; in every group one owner receives exactly 2 pages from every source.
All inputs are finite; a program needn't handle non-finite values.
Results may differ from a plain program's by a relative error of at most 0.0063.
Values may be sent and summed in bfloat16 or wider, within the bound.
No kernel may reach another device: no remote copies, remote signals or barrier semaphores. Data moves between devices by JAX's collectives and lax.ppermute only.
A program may use at most 64 MiB of HBM per device.

v0:
```python
import jax
import jax.numpy as jnp
from jax import lax
from jax.sharding import PartitionSpec as P

HEAD_DIM = 128
IMAGE_PAGES = 32


query_scale = 1.0 / 12.0
softcap = 50.0
epsilon = 1e-06


def laid_out(parts, dim):
    parts = jnp.moveaxis(parts, 0, dim)
    lengths = parts.shape
    return parts.reshape(*lengths[:dim], lengths[dim] * lengths[dim + 1], *lengths[dim + 2 :])


def sent_to_all(x, axis):
    copies = jnp.broadcast_to(x, (lax.axis_size(axis), *x.shape))
    return lax.all_to_all(copies, axis, split_axis=0, concat_axis=0, tiled=True)


def gather_directly(x, axis, dim):
    return laid_out(sent_to_all(x, axis), dim)


def over_copies(x, axis):
    everything = sent_to_all(x, axis)
    return jnp.sum(everything, axis=0)


def cut_along(x, dim, devices):
    before, after = (x.shape[:dim], x.shape[dim + 1 :])
    return jnp.moveaxis(x.reshape(*before, devices, -1, *after), dim, 0)


def summed_on_arrival(x, axis, dim):
    devices = lax.axis_size(axis)
    parts = lax.all_to_all(cut_along(x, dim, devices), axis, 0, 0, tiled=True)
    return jnp.sum(parts, axis=0)


def from_behind(value, axis, steps):
    count = lax.axis_size(axis)
    pairs = [(source, (source + steps) % count) for source in range(count)]
    return lax.ppermute(value, axis, pairs)


def together(arrays, axis):
    ends = [0]
    for a in arrays:
        ends.append(ends[-1] + a.size)
    subtotal = over_copies(jnp.concatenate([a.ravel() for a in arrays]), axis)
    return tuple((subtotal[b:e].reshape(a.shape) for a, b, e in zip(arrays, ends, ends[1:])))


def block_ranks(owners):
    per_block = owners.shape[1]
    same_owner = owners[:, :, None] == owners[:, None, :]
    earlier = jnp.arange(per_block)[None, :] < jnp.arange(per_block)[:, None]
    return jnp.sum((same_owner & earlier[None, :, :]).astype(jnp.int32), axis=2)


def attend_part(query_grid, page_store, token_mask):
    slot_count = page_store.shape[0]
    page_len = page_store.shape[1]
    head_count = page_store.shape[3] // HEAD_DIM
    keys = page_store[:, :, 0, :].reshape(slot_count * page_len, head_count, HEAD_DIM)
    values = page_store[:, :, 1, :].reshape(slot_count * page_len, head_count, HEAD_DIM)
    raw_scores = jnp.einsum("rkgd,tkd->rkgt", query_grid, keys, preferred_element_type=jnp.float32)
    capped = softcap * jnp.tanh(raw_scores * query_scale / softcap)
    allowed = token_mask.reshape(slot_count * page_len, -1).T
    weights = jnp.where(allowed[:, None, None, :], jnp.exp(capped), jnp.float32(0.0))
    totals = jnp.sum(weights, axis=3)
    weighted = jnp.einsum(
        "rkgt,tkd->rkgd", weights.astype(jnp.bfloat16), values, preferred_element_type=jnp.float32
    )
    return (totals, weighted)


def per_device(
    patches,
    vis_gain,
    vis_bias,
    w_proj,
    b_proj,
    rms_gain,
    w_kv,
    queries,
    cache,
    cache_lengths,
    slot_page,
    page_owner,
    image_request,
):
    kv_count = lax.axis_size("kv")
    section_idx = lax.axis_index("section")
    kv_idx = lax.axis_index("kv")
    row_count = patches.shape[0]
    page_len = cache.shape[1]
    pages_dev = row_count // page_len
    capacity = max(2, (2 * pages_dev + kv_count - 1) // kv_count)
    recv_slots = kv_count * capacity
    gathered = gather_directly(patches, "tp", 1).astype(jnp.float32)
    row_mean = jnp.mean(gathered, axis=1, keepdims=True)
    centred = gathered - row_mean
    variance = jnp.mean(centred * centred, axis=1, keepdims=True)
    x_norm = (centred * lax.rsqrt(variance + epsilon) * vis_gain + vis_bias).astype(jnp.bfloat16)
    projected = (
        jnp.dot(
            x_norm,
            lax.all_gather(w_proj, "section", axis=0, tiled=True),
            preferred_element_type=jnp.float32,
        )
        + b_proj
    )
    squares = over_copies(jnp.sum(projected * projected, axis=1), "tp")
    full_width = projected.shape[1] * lax.axis_size("tp")
    hidden = (projected * lax.rsqrt(squares / full_width + epsilon)[:, None] * rms_gain).astype(
        jnp.bfloat16
    )
    partial_kv = jnp.einsum("nd,dcf->ncf", hidden, w_kv, preferred_element_type=jnp.float32)
    image_kv = summed_on_arrival(partial_kv, "tp", 2)
    kv_pages = image_kv.astype(jnp.bfloat16).reshape(pages_dev, page_len, 2, image_kv.shape[2])
    handed = from_behind(kv_pages, "section", 1)
    owners = lax.dynamic_index_in_dim(page_owner, section_idx, 0, keepdims=False).reshape(
        kv_count, pages_dev
    )
    page_ranks = block_ranks(owners)
    my_owner = lax.dynamic_index_in_dim(owners, kv_idx, 0, keepdims=False)
    my_rank = lax.dynamic_index_in_dim(page_ranks, kv_idx, 0, keepdims=False)
    target = my_owner * capacity + my_rank
    placing = (jnp.arange(recv_slots)[:, None] == target[None, :]).astype(jnp.bfloat16)
    new_pages = lax.all_to_all(
        jnp.einsum("jp,ptcf->jtcf", placing, handed, preferred_element_type=jnp.float32).astype(
            jnp.bfloat16
        ),
        "kv",
        split_axis=0,
        concat_axis=0,
        tiled=True,
    )
    req_count = queries.shape[0]
    kv_heads_dev = cache.shape[3] // HEAD_DIM
    group_size = queries.shape[1] // HEAD_DIM // kv_heads_dev
    query_grid = queries.reshape(req_count, kv_heads_dev, group_size, HEAD_DIM)
    lengths = cache_lengths[0]
    page_counts = (lengths + page_len - 1) // page_len
    starts = jnp.cumsum(page_counts) - page_counts
    slot_ids = slot_page[0]
    within = slot_ids[:, None] - starts[None, :]
    inside = (within >= 0) & (within < page_counts[None, :])
    valid = jnp.where(inside, jnp.clip(lengths[None, :] - within * page_len, 0, page_len), 0)
    cache_mask = jnp.arange(page_len)[None, :, None] < valid[:, None, :]
    cache_totals, cache_weighted = attend_part(query_grid, cache, cache_mask)
    own_owners = lax.dynamic_index_in_dim(page_owner, section_idx, 0, keepdims=False).reshape(
        kv_count, pages_dev
    )
    own_ranks = block_ranks(own_owners)
    slot_of = (jnp.arange(kv_count)[:, None] * capacity + own_ranks).reshape(-1)
    arrives_here = own_owners.reshape(-1) == kv_idx
    image_count = image_request.shape[1]
    image_of = jnp.arange(kv_count * pages_dev) // IMAGE_PAGES
    request_row = image_request[0]
    page_request = jnp.sum(
        jnp.where(image_of[:, None] == jnp.arange(image_count)[None, :], request_row[None, :], 0),
        axis=1,
    )
    matched = arrives_here[None, :] & (slot_of[None, :] == jnp.arange(recv_slots)[:, None])
    request_hit = page_request[:, None] == jnp.arange(req_count)[None, :]
    slot_request = jnp.any(matched[:, :, None] & request_hit[None, :, :], axis=1)
    image_mask = jnp.broadcast_to(slot_request[:, None, :], (recv_slots, page_len, req_count))
    image_totals, image_weighted = attend_part(query_grid, new_pages, image_mask)
    totals, weighted = together(
        (cache_totals + image_totals, cache_weighted + image_weighted), "kv"
    )
    attended = (weighted / totals[..., None]).astype(jnp.bfloat16).reshape(req_count, -1)
    return (new_pages, attended)


def solution(mesh):
    in_specs = (
        P(("section", "kv"), "tp"),
        P(),
        P(),
        P("section", "tp"),
        P("tp"),
        P("tp"),
        P("tp", None, None),
        P("section", "tp"),
        P(("section", "kv"), None, None, "tp"),
        P("section", None),
        P("section", "kv"),
        P(),
        P("section", None),
    )
    out_specs = (P(("section", "kv"), None, None, "tp"), P("section", "tp"))
    return jax.shard_map(
        per_device, mesh=mesh, in_specs=in_specs, out_specs=out_specs, check_vma=False
    )
```

profile of v0, /device:TPU:2, one launch (start us, length us, event | category | flops | bytes accessed | tf_op | source)
XLA Modules:
  0.0 313.6 jit_solution(7396003237262253135)
XLA Ops:
  7.2 0.7 all-gather.2.cloned.1.call-update
  7.9 1.0 broadcast_in_dim.44
  9.0 19.7 %all_to_all.27 = bf16[4,512,288]{1,2,0:T(8,128)(2,1)S(1)} all-to-all(bf16[4,512,288]{1,2,0:T(8,128)(2,1)S(1)} %broadcast_in_dim.44), channel_id=1, replica_groups=mesh['section'=4,'kv'=16,'tp'=4] {'tp'}, dimensions={0} | all-to-all | bytes 2359296 | tf_op jit(solution)/shard_map/all_to_all | solution.py:23
  28.7 0.2 convert_reduce_fusion
  28.9 0.4 multiply_reduce_fusion.1
  29.3 0.5 fusion.10
  29.8 32.4 %all-gather.2.cloned.1.call-done = bf16[1152,1152]{1,0:T(8,128)(2,1)} async-done(((bf16[288,1152]{1,0:T(8,128)(2,1)}), bf16[1152,1152]{1,0:T(8,128)(2,1)}) %all-gather.2.cloned.1.call-update) | async-done | bytes 2654224 | tf_op jit(solution)/shard_map/all_gather | solution.py:115
  62.2 3.8 %multiply_reduce_fusion = (f32[512]{0:T(512)S(1)}, f32[512,1152]{1,0:T(8,128)S(1)}) fusion(f32[1152]{0:T(1024)S(1)} %copy-done.2, bf16[512,1152]{0,1:T(8,128)(2,1)S(1)} %fusion.10, bf16[1152,1152]{1,0:T(8,128)(2,1)} %all-gather.2.cloned.1.call-done), kind=kOutput, calls=%fused_computation.19 | convolution fusion | flops 1360723456 | bytes 6199808 | tf_op jit(solution)/shard_map/dot_general | solution.py:113
  66.0 8.5 %all_to_all.28 = f32[4,1,512]{2,1,0:T(1,128)S(1)} all-to-all(f32[4,1,512]{2,1,0:T(1,128)S(1)} %broadcast_in_dim.45), channel_id=1, replica_groups=mesh['section'=4,'kv'=16,'tp'=4] {'tp'}, dimensions={0} | all-to-all | bytes 16384 | tf_op jit(solution)/shard_map/all_to_all | solution.py:23
  74.5 5.3 %fusion = f32[512,2,1024]{2,0,1:T(8,128)S(1)} fusion(bf16[1152,2,1024]{2,1,0:T(2,128)(2,1)} %param.19, f32[512,1152]{1,0:T(8,128)S(1)} %get-tuple-element.11, f32[1152]{0:T(1024)} %param.18, f32[512]{0:T(512)S(1)} %add_rsqrt_fusion), kind=kOutput, calls=%fused_computation | convolution fusion | flops 2417688576 | bytes 11278848 | tf_op jit(solution)/shard_map/nd,dcf->ncf/dot_general | solution.py:125
  79.8 0.4 copy.163
  80.2 51.5 %all_to_all.29 = f32[4,512,2,256]{3,1,2,0:T(8,128)} all-to-all(f32[4,512,2,256]{3,1,2,0:T(8,128)S(1)} %bitcast.89), channel_id=1, replica_groups=mesh['section'=4,'kv'=16,'tp'=4] {'tp'}, dimensions={0} | all-to-all | bytes 8388608 | tf_op jit(solution)/shard_map/all_to_all | solution.py:42
  131.7 2.5 reduce_sum.99
  134.2 0.4 copy.96
  134.6 0.3 collective-permute-start
  134.9 0.1 reshape.263
  135.0 0.1 copy.90
  135.1 0.1 convert_reduce_fusion.1
  135.2 0.2 add_reduce_fusion
  135.4 17.6 %collective-permute-done = bf16[4,128,2,256]{3,0,2,1:T(4,128)(2,1)S(1)} collective-permute-done((bf16[4,128,2,256]{3,0,2,1:T(4,128)(2,1)S(1)}, bf16[4,128,2,256]{3,0,2,1:T(4,128)(2,1)S(1)}, u32[]{:S(2)}, u32[]{:S(2)}) %collective-permute-start) | collective-permute-done | bytes 524320 | tf_op jit(solution)/shard_map/ppermute | solution.py:49
  153.0 1.4 convolution_convert_fusion
  154.3 6.3 %copy.97 = bf16[32,128,2,256]{3,2,1,0:T(2,128)(2,1)} copy(bf16[32,128,2,256]{3,0,2,1:T(8,128)(2,1)S(1)} %convolution_convert_fusion) | data formatting | bytes 8388608 | tf_op jit(solution)/shard_map/convert_element_type | solution.py:138
  160.7 4.9 %all-to-all-start.3 = ((bf16[32,128,2,256]{3,2,1,0:T(2,128)(2,1)}), bf16[32,128,2,256]{3,2,1,0:T(2,128)(2,1)}, u32[]{:S(2)}, u32[]{:S(2)}) async-start(bf16[32,128,2,256]{3,2,1,0:T(2,128)(2,1)} %copy.97), calls=%async_computation.3 | async-start | bytes 8388608 | tf_op jit(solution)/shard_map/all_to_all | solution.py:137
  165.6 0.1 copy.101
  165.7 0.1 add.113
  165.8 0.1 fusion.41
  165.9 0.2 and_reduce_fusion
  166.1 0.1 broadcast_bitcast_fusion
  166.2 10.0 %slice_reduce_fusion.3 = (bf16[16,128,256]{2,1,0:T(8,128)(2,1)}, bf16[16,128,256]{2,1,0:T(8,128)(2,1)S(1)}) fusion(bf16[16,128,2,256]{3,2,1,0:T(2,128)(2,1)S(1)} %copy-done.1), kind=kLoop, calls=%fused_computation.31 | loop fusion | bytes 4194304 | tf_op jit(solution)/shard_map/slice | solution.py:71
  176.2 1.4 reshape.276
  177.6 0.2 reduce-window_clone.1
  177.8 0.3 reshape.278
  178.1 0.1 fusion.37
  178.3 0.5 fusion.44
  178.8 0.3 convolution_bitcast_fusion
  179.0 60.3 %all-to-all-done.3 = bf16[32,128,2,256]{3,2,1,0:T(2,128)(2,1)} async-done(((bf16[32,128,2,256]{3,2,1,0:T(2,128)(2,1)}), bf16[32,128,2,256]{3,2,1,0:T(2,128)(2,1)}, u32[]{:S(2)}, u32[]{:S(2)}) %all-to-all-start.3) | async-done | bytes 4194336 | tf_op jit(solution)/shard_map/all_to_all | solution.py:137
  239.3 21.9 %slice_reduce_fusion.1 = (bf16[32,128,256]{2,1,0:T(8,128)(2,1)S(1)}, bf16[32,128,256]{2,1,0:T(8,128)(2,1)}) fusion(bf16[32,128,2,256]{3,2,1,0:T(2,128)(2,1)} %all-to-all-done.3), kind=kLoop, calls=%fused_computation.10 | loop fusion | bytes 8388608 | tf_op jit(solution)/shard_map/slice | solution.py:71
  261.2 2.1 reshape.277
  263.3 2.5 reshape.279
  265.8 2.3 fusion.45
  268.2 0.4 fusion.26
  268.6 0.1 copy.105
  268.7 0.1 add.115
  269.0 27.6 %all_to_all.30 = f32[16,1,2064]{2,1,0:T(1,128)S(1)} all-to-all(f32[16,1,2064]{2,1,0:T(1,128)S(1)} %broadcast_in_dim.54), channel_id=1, replica_groups=mesh['section'=4,'kv'=16,'tp'=4] {'kv'}, dimensions={0} | all-to-all | bytes 264192 | tf_op jit(solution)/shard_map/all_to_all | solution.py:23
  296.5 0.1 reduce_sum.103
  296.7 0.1 div.69
  296.9 0.6 divide_convert_fusion
  297.5 9.2 %copy.166 = bf16[32,128,2,256]{3,2,1,0:T(2,128)(2,1)} copy(bf16[32,128,2,256]{3,2,1,0:T(2,128)(2,1)} %all-to-all-done.3) | data formatting | bytes 8388608
  (48 shorter events, 0.7 us)
Async XLA Ops:
  7.2 171.1 %copy-start = (bf16[4,512]{1,0:T(4,128)(2,1)S(1)}, bf16[4,512]{1,0:T(4,128)(2,1)}, u32[]{:S(2)}) copy-start(bf16[4,512]{1,0:T(4,128)(2,1)} %param.20) | copy-start | bytes 12292
  7.2 55.0 %all-gather.2.cloned.1.call-start = ((), (), s32[]{:S(2)}) async-start(), calls=%async_computation.5 | async-start | bytes 3317760 | tf_op jit(solution)/shard_map/all_gather | solution.py:115
  9.0 20.3 %copy-start.3 = (f32[1152]{0:T(1024)S(1)}, f32[1152]{0:T(1024)}, u32[]{:S(2)}) copy-start(f32[1152]{0:T(1024)} %param.15) | copy-start | bytes 13828
  9.0 20.3 %copy-start.4 = (f32[1152]{0:T(1024)S(1)}, f32[1152]{0:T(1024)}, u32[]{:S(2)}) copy-start(f32[1152]{0:T(1024)} %param.14) | copy-start | bytes 13828
  28.7 33.5 %copy-start.2 = (f32[1152]{0:T(1024)S(1)}, f32[1152]{0:T(1024)}, u32[]{:S(2)}) copy-start(f32[1152]{0:T(1024)} %param.17) | copy-start | bytes 13828
  131.6 3.2 %copy-start.7 = (s32[4,64]{1,0:T(4,128)S(1)}, s32[4,64]{1,0:T(4,128)}, u32[]{:S(2)}) copy-start(s32[4,64]{1,0:T(4,128)} %param.24) | copy-start | bytes 3076
  134.6 18.4 %collective-permute-start = (bf16[4,128,2,256]{3,0,2,1:T(4,128)(2,1)S(1)}, bf16[4,128,2,256]{3,0,2,1:T(4,128)(2,1)S(1)}, u32[]{:S(2)}, u32[]{:S(2)}) collective-permute-start(bf16[4,128,2,256]{3,0,2,1:T(4,128)(2,1)S(1)} %copy.96), channel_id=1, source_target_pairs={{0,64},{64,128},{128,192},{192,0},{1,65},{65,129},{129,193},{193,1... | collective-permute-start | bytes 1572872 | tf_op jit(solution)/shard_map/ppermute | solution.py:49
  160.7 5.1 %copy-start.8 = (s32[1,2]{1,0:T(1,128)S(1)}, s32[1,2]{1,0:T(1,128)}, u32[]{:S(2)}) copy-start(s32[1,2]{1,0:T(1,128)} %param.25) | copy-start | bytes 28
  160.7 5.5 %copy-start.1 = (bf16[16,128,2,256]{3,2,1,0:T(2,128)(2,1)S(1)}, bf16[16,128,2,256]{3,2,1,0:T(2,128)(2,1)}, u32[]{:S(2)}) copy-start(bf16[16,128,2,256]{3,2,1,0:T(2,128)(2,1)} %param.21) | copy-start | bytes 6291460
  160.7 78.6 %all-to-all-start.3 = ((bf16[32,128,2,256]{3,2,1,0:T(2,128)(2,1)}), bf16[32,128,2,256]{3,2,1,0:T(2,128)(2,1)}, u32[]{:S(2)}, u32[]{:S(2)}) async-start(bf16[32,128,2,256]{3,2,1,0:T(2,128)(2,1)} %copy.97), calls=%async_computation.3 | async-start | bytes 8388608 | tf_op jit(solution)/shard_map/all_to_all | solution.py:137
  166.2 11.3 %copy-start.5 = (s32[1,4]{1,0:T(1,128)S(1)}, s32[1,4]{1,0:T(1,128)}, u32[]{:S(2)}) copy-start(s32[1,4]{1,0:T(1,128)} %param.22) | copy-start | bytes 52
  176.2 1.9 copy-start.6
Sparse Core Ops, SparseCore 0:
  9.8 52.3 all-gather.1
where the time goes:
time: 314 us
  waiting for transfers between devices  111 us (35%)
  blocking collectives  107 us (34%)
  local copies, waits for them, and re-layouts  56.6 us (18%)
  between operations  14.4 us (5%)
  matrix products  14 us (4%)
  other arithmetic  5.3 us (2%)
  starting transfers between devices  5.19 us (2%)
    all_to_all x1, waiting for transfers between devices, per_device(): lax.all_to_all(jnp.einsum('jp,ptcf->jtcf', placing, handed, preferred_ele...  60.3 us
    all_to_all x3, blocking collectives, sent_to_all(): return lax.all_to_all(copies, axis, split_axis=0, concat_axis=0, tiled=True)  55.7 us
    all_to_all x1, blocking collectives, summed_on_arrival(): parts = lax.all_to_all(cut_along(x, dim, devices), axis, 0, 0, tiled=True)  51.5 us
    all_gather x1, waiting for transfers between devices, per_device(): lax.all_gather(w_proj, 'section', axis=0, tiled=True)  32.4 us
    slice x2, local copies, waits for them, and re-layouts, attend_part(): page_store[:, :, 0, :].reshape(slot_count * page_len, head_count, HEAD_DIM)  31.9 us
    ppermute x1, waiting for transfers between devices, from_behind(): return lax.ppermute(value, axis, pairs)  17.6 us
    unnamed x22, local copies, waits for them, and re-layouts  9.42 us
    convert_element_type x1, local copies, waits for them, and re-layouts, per_device(): jnp.einsum('jp,ptcf->jtcf', placing, handed, preferred_element_type=jnp.f...  6.33 us
  transfers between devices with their start and end apart: 3, of which 3 were waited for; matrix products, arithmetic and copies ran while one was open for 5% of the time, Pallas kernels for 0%

commit v1 on v0

v1 whole, which is shorter than its diff:
```python
import functools

import jax
import jax.numpy as jnp
from jax import lax
from jax.experimental import pallas as pl
from jax.experimental.pallas import tpu as pltpu
from jax.sharding import Mesh, PartitionSpec as P

HEAD_DIM = 128
IMAGE_PAGES = 32
PAGE = 128

query_scale = 1.0 / 12.0
softcap = 50.0
epsilon = 1e-06


def block_ranks(owners):
    per_block = owners.shape[1]
    same_owner = owners[:, :, None] == owners[:, None, :]
    earlier = jnp.arange(per_block)[None, :] < jnp.arange(per_block)[:, None]
    return jnp.sum((same_owner & earlier[None, :, :]).astype(jnp.int32), axis=2)


def attend_part(query_grid, keys, values, allowed):
    raw_scores = jnp.einsum("rkgd,tkd->rkgt", query_grid, keys, preferred_element_type=jnp.float32)
    capped = softcap * jnp.tanh(raw_scores * query_scale / softcap)
    weights = jnp.where(allowed[:, None, None, :], jnp.exp(capped), jnp.float32(0.0))
    totals = jnp.sum(weights, axis=3)
    weighted = jnp.einsum(
        "rkgt,tkd->rkgd", weights.astype(jnp.bfloat16), values, preferred_element_type=jnp.float32
    )
    return (totals, weighted)


def encode_kernel(order, x_own, x_left, x_right, x_far, w_own, w_core, w_half, w_both,
                  gain, bias, b_proj, rms_gain, w_kv, out, squares, xs, ws, sems):
    rows = x_own.shape[0]
    copies = []
    for i, ref in enumerate((x_own, x_left, x_right, x_far)):
        copies.append(pltpu.make_async_copy(ref, xs.at[order[i]], sems.at[i]))
    for i, ref in enumerate((w_own, w_core, w_half, w_both)):
        copies.append(pltpu.make_async_copy(ref, ws.at[order[4 + i]], sems.at[4 + i]))
    for c in copies:
        c.start()
    for c in copies:
        c.wait()
    step = 128
    width = 4 * xs.shape[2]

    def body(i, carry):
        at = pl.ds(pl.multiple_of(i * step, step), step)
        parts = [xs[j, at, :].astype(jnp.float32) for j in range(4)]
        mean = sum(jnp.sum(p, axis=1, keepdims=True) for p in parts) / width
        parts = [p - mean for p in parts]
        var = sum(jnp.sum(p * p, axis=1, keepdims=True) for p in parts) / width
        inv = lax.rsqrt(var + epsilon)
        acc = None
        for j in range(4):
            xn = (parts[j] * inv * gain[j] + bias[j]).astype(jnp.bfloat16)
            d = jnp.dot(xn, ws[j], preferred_element_type=jnp.float32)
            acc = d if acc is None else acc + d
        projected = acc + b_proj[...]
        sq = jnp.sum(projected * projected, axis=1, keepdims=True)
        squares[:, at] = jnp.transpose(jnp.broadcast_to(sq, (step, 128)))[:8]
        hidden = (projected * rms_gain[...]).astype(jnp.bfloat16)
        res = jnp.dot(hidden, w_kv[...], preferred_element_type=jnp.float32).astype(jnp.bfloat16)
        for t in range(4):
            out[t, at, 0:256] = res[:, t * 256 : (t + 1) * 256]
            out[t, at, 256:512] = res[:, 1024 + t * 256 : 1024 + (t + 1) * 256]
        return carry

    lax.fori_loop(0, rows // step, body, 0)


def encode(order, xs, ws, gain, bias, b_proj, rms_gain, w_kv):
    rows = xs[0].shape[0]
    any_spec = pl.BlockSpec(memory_space=pl.ANY)
    vmem = pl.BlockSpec(memory_space=pltpu.VMEM)
    return pl.pallas_call(
        encode_kernel,
        out_shape=(
            jax.ShapeDtypeStruct((4, rows, 512), jnp.bfloat16),
            jax.ShapeDtypeStruct((8, rows), jnp.float32),
        ),
        in_specs=[pl.BlockSpec(memory_space=pltpu.SMEM)] + [any_spec] * 8 + [vmem] * 5,
        out_specs=(vmem, vmem),
        scratch_shapes=[
            pltpu.VMEM((4, rows, 288), jnp.bfloat16),
            pltpu.VMEM((4, 288, 1152), jnp.bfloat16),
            pltpu.SemaphoreType.DMA((8,)),
        ],
        compiler_params=pltpu.CompilerParams(vmem_limit_bytes=40 << 20),
        name="encode",
    )(order, *xs, *ws, gain, bias, b_proj, rms_gain, w_kv)


def pick_kernel(code, first, second, zero, out, sem):
    for i in range(8):
        c = code[i]

        @pl.when(c < 0)
        def _():
            pltpu.make_async_copy(zero, out.at[i], sem).start()

        @pl.when((c >= 0) & (c < 4))
        def _():
            pltpu.make_async_copy(first.at[c], out.at[i], sem).start()

        @pl.when(c >= 4)
        def _():
            pltpu.make_async_copy(second.at[c - 4], out.at[i], sem).start()

    for i in range(8):
        pltpu.make_async_copy(zero, out.at[i], sem).wait()


def pick(code, first, second, zero):
    any_spec = pl.BlockSpec(memory_space=pl.ANY)
    return pl.pallas_call(
        pick_kernel,
        out_shape=jax.ShapeDtypeStruct((8,) + first.shape[1:], first.dtype),
        in_specs=[pl.BlockSpec(memory_space=pltpu.SMEM), any_spec, any_spec, any_spec],
        out_specs=any_spec,
        scratch_shapes=[pltpu.SemaphoreType.DMA],
        name="pick",
    )(code, first, second, zero)


def per_device(
    patches, vis_gain, vis_bias, w_proj, b_proj, rms_gain, w_kv, queries, cache,
    cache_lengths, slot_page, page_owner, image_request,
):
    zh, co, zl = lax.axis_index("zh"), lax.axis_index("co"), lax.axis_index("zl")
    y, tp = lax.axis_index("y"), lax.axis_index("tp")
    section = zh * 2 + co

    hop = []
    for a in range(2):
        for z in range(4):
            hop.append((a * 8 + z, a * 8 + 4 + z))
            hop.append((a * 8 + 4 + z, (1 - a) * 8 + (z ^ 2)))
    x_own = lax.ppermute(patches, ("zh", "co", "zl"), hop)

    swap = [(0, 1), (1, 0)]
    w_core = lax.ppermute(w_proj, "co", swap)
    piece_rows = w_proj.shape[0] // 4
    piece = lax.dynamic_slice_in_dim(w_proj, y * piece_rows, piece_rows, 0)
    cross = [(a * 4 + z, (1 - a) * 4 + (z ^ 2)) for a in range(2) for z in range(4)]
    piece = lax.ppermute(piece, ("zh", "zl"), cross)
    ring = lambda n: [(i, (i + n) % 4) for i in range(4)]
    p1 = lax.ppermute(piece, "y", ring(1))
    p3 = lax.ppermute(piece, "y", ring(3))
    p2 = lax.ppermute(piece, "y", ring(2))
    w_half = jnp.zeros((4,) + piece.shape, piece.dtype)
    for k, p in ((0, piece), (1, p1), (2, p2), (3, p3)):
        w_half = lax.dynamic_update_index_in_dim(w_half, p, (y - k) % 4, 0)
    w_half = w_half.reshape(w_proj.shape)
    w_both = lax.ppermute(w_half, "co", swap)

    half = x_own.shape[0] // 2
    x_left = lax.ppermute(x_own, "tp", ring(1))
    x_right = lax.ppermute(x_own, "tp", ring(3))
    far_a = lax.ppermute(x_left[:half], "tp", ring(1))
    far_b = lax.ppermute(x_right[half:], "tp", ring(3))
    x_far = jnp.concatenate([far_a, far_b], axis=0)

    order = jnp.stack(
        [tp, (tp + 3) % 4, (tp + 1) % 4, (tp + 2) % 4, section, section ^ 1, section ^ 2, section ^ 3]
    ).astype(jnp.int32)
    w_kv2 = w_kv.reshape(w_kv.shape[0], -1)
    partial, squares = encode(
        order, (x_own, x_left, x_right, x_far), (w_proj, w_core, w_half, w_both),
        vis_gain.reshape(4, 1, 288), vis_bias.reshape(4, 1, 288),
        b_proj.reshape(1, -1), rms_gain.reshape(1, -1), w_kv2,
    )
    total_sq = squares
    for n in (1, 3, 2):
        total_sq = total_sq + lax.ppermute(squares, "tp", ring(n))
    scale = lax.rsqrt(total_sq[0] / (b_proj.shape[0] * 4) + epsilon)
    parts = lax.all_to_all(partial, "tp", 0, 0, tiled=True)
    summed = jnp.sum(parts.astype(jnp.float32), axis=0)
    image_kv = (summed * scale[:, None]).astype(jnp.bfloat16)
    pages = jnp.stack(
        [image_kv[:, :256].reshape(4, PAGE, 256), image_kv[:, 256:].reshape(4, PAGE, 256)], axis=2
    )

    owners = lax.dynamic_index_in_dim(page_owner, section, 0, keepdims=False).reshape(16, 4)
    ranks = block_ranks(owners)
    flip = jnp.where(co == 0, 2, 0)
    first3 = jnp.stack([zl, zl ^ 1, jnp.where(zl < 2, 2, 1), jnp.where(zl < 2, 3, 0)])
    z_src = first3 ^ flip
    k_src = z_src * 4 + y
    own_rows = owners[k_src]
    rank_rows = ranks[k_src]
    want_owner = (zl * 4 + jnp.arange(8) // 2)[None, :, None]
    want_rank = (jnp.arange(8) % 2)[None, :, None]
    match = (own_rows[:, None, :] == want_owner) & (rank_rows[:, None, :] == want_rank)
    code = jnp.sum(jnp.where(match, jnp.arange(4)[None, None, :] + 1, 0), axis=2) - 1
    middle = (zl == 1) | (zl == 2)
    shift = jnp.where(middle, 0, 4) * jnp.array([0, 0, 1, 1])
    code = jnp.where(code >= 0, code + shift[:, None], -1).astype(jnp.int32)

    zero = jnp.zeros((PAGE, 2, 256), jnp.bfloat16)
    pair = [(0, 1), (1, 0), (2, 3), (3, 2)]
    mid = [(1, 2), (2, 1)]
    outer = [(1, 0), (2, 3)]
    b1 = lax.ppermute(pages, "zl", pair)
    b2m = lax.ppermute(pages, "zl", mid)
    b3m = lax.ppermute(b1, "zl", mid)
    b2o = lax.ppermute(b2m, "zl", outer)
    b3o = lax.ppermute(b3m, "zl", outer)
    new_pages = jnp.zeros((32, PAGE, 2, 256), jnp.bfloat16)
    for i, (f, s) in enumerate(((pages, pages), (b1, b1), (b2m, b2o), (b3m, b3o))):
        sent = pick(code[i], f, s, zero)
        got = lax.all_to_all(sent, "y", 0, 0, tiled=True)
        new_pages = lax.dynamic_update_slice_in_dim(new_pages, got, z_src[i] * 8, 0)

    req_count = queries.shape[0]
    query_grid = queries.reshape(req_count, 2, 2, HEAD_DIM)
    lengths = cache_lengths[0]
    page_counts = (lengths + PAGE - 1) // PAGE
    starts = jnp.cumsum(page_counts) - page_counts
    within = slot_page[0][:, None] - starts[None, :]
    inside = (within >= 0) & (within < page_counts[None, :])
    valid = jnp.where(inside, jnp.clip(lengths[None, :] - within * PAGE, 0, PAGE), 0)
    cache_mask = jnp.arange(PAGE)[None, :, None] < valid[:, None, :]
    keys = cache[:, :, 0, :].reshape(-1, 2, HEAD_DIM)
    values = cache[:, :, 1, :].reshape(-1, 2, HEAD_DIM)
    c_tot, c_num = attend_part(query_grid, keys, values, cache_mask.reshape(-1, req_count).T)
    my_request = lax.dynamic_index_in_dim(image_request[0], (zl ^ flip) // 2, 0, keepdims=False)
    i_mask = jnp.broadcast_to((jnp.arange(req_count) == my_request)[:, None], (req_count, image_kv.shape[0]))
    i_tot, i_num = attend_part(
        query_grid, image_kv[:, :256].reshape(-1, 2, HEAD_DIM), image_kv[:, 256:].reshape(-1, 2, HEAD_DIM), i_mask
    )
    tot = (c_tot + i_tot).reshape(16)
    num = (c_num + i_num).reshape(16, HEAD_DIM)
    both = jnp.concatenate([num, jnp.broadcast_to(tot[:, None], num.shape)], axis=0)
    for axis in ("y", "zl"):
        for m in (1, 2):
            both = both + lax.ppermute(both, axis, [(i, i ^ m) for i in range(4)])
    attended = (both[:16] / both[16:]).astype(jnp.bfloat16).reshape(req_count, -1)
    return (new_pages, attended)


def solution(mesh):
    fine = Mesh(mesh.devices.reshape(2, 2, 4, 4, 4), ("zh", "co", "zl", "y", "tp"))
    sec, kv, every = ("zh", "co"), ("zl", "y"), ("zh", "co", "zl", "y")
    in_specs = (
        P(every, "tp"), P(), P(), P(sec, "tp"), P("tp"), P("tp"), P("tp", None, None), P(sec, "tp"),
        P(every, None, None, "tp"), P(sec, None), P(sec, kv), P(), P(sec, None),
    )
    out_specs = (P(every, None, None, "tp"), P(sec, "tp"))
    return jax.shard_map(per_device, mesh=fine, in_specs=in_specs, out_specs=out_specs, check_vma=False)
```

time: 314 us -> 323 us (1.029)
  Pallas kernels: 0 us -> 145 us
  blocking collectives: 107 us -> 0 us
  waiting for transfers between devices: 111 us -> 47.8 us
  starting transfers between devices: 5.19 us -> 61.2 us
  between operations: 14.4 us -> 3.79 us
  matrix products: 14 us -> 3.61 us
  local copies, waits for them, and re-layouts: 56.6 us -> 52.2 us
    pallas_call x0 -> x5, Pallas kernels: none -> 145 us  [the longest x4 134 us: pick(): pl.pallas_call(pick_kernel, out_shape=jax.ShapeDtypeStruct((8,) + first.s...]
    all_to_all x4 -> x0, blocking collectives: 107 us -> none  [the longest x3 55.7 us: sent_to_all(): return lax.all_to_all(copies, axis, split_axis=0, concat_axis=0, tiled=True)]
    all_to_all x1 -> x5, waiting for transfers between devices: 60.3 us -> 0.01 us  [the longest x4 0.01 us: per_device(): got = lax.all_to_all(sent, 'y', 0, 0, tiled=True)]
    ppermute x1 -> x23, starting transfers between devices: 0.26 us -> 34 us  [the longest x4 7.29 us: per_device(): both = both + lax.ppermute(both, axis, [(i, i ^ m) for i in range(4)])]
    all_gather x1 -> x0, waiting for transfers between devices: 32.4 us -> none  [per_device(): lax.all_gather(w_proj, 'section', axis=0, tiled=True)]
    ppermute x1 -> x23, waiting for transfers between devices: 17.6 us -> 47.8 us  [the longest x1 10.6 us: per_device(): b1 = lax.ppermute(pages, 'zl', pair)]
    all_to_all x1 -> x5, starting transfers between devices: 4.89 us -> 27.2 us  [the longest x4 19.7 us: per_device(): got = lax.all_to_all(sent, 'y', 0, 0, tiled=True)]
    slice x4 -> x7, local copies, waits for them, and re-layouts: 32 us -> 12.2 us  [the longest x1 9.85 us: per_device(): keys = cache[:, :, 0, :].reshape(-1, 2, HEAD_DIM)]
  transfers between devices with their start and end apart: 3 -> 28, of which waited for: 3 -> 9; matrix products, arithmetic and copies ran while one was open for 5% -> 15% of each run, Pallas kernels for 0% -> 31%
where the time goes in v1:
time: 323 us; the launch traced here: 321 us
  Pallas kernels  145 us (45%)
  starting transfers between devices  61.2 us (19%)
  local copies, waits for them, and re-layouts  52.2 us (16%)
  waiting for transfers between devices  47.8 us (15%)
  other arithmetic  7.35 us (2%)
  between operations  3.79 us (1%)
  matrix products  3.61 us (1%)
    pallas_call x4, Pallas kernels, pick(): pl.pallas_call(pick_kernel, out_shape=jax.ShapeDtypeStruct((8,) + first.s...  134 us
    all_to_all x4, starting transfers between devices, per_device(): got = lax.all_to_all(sent, 'y', 0, 0, tiled=True)  19.7 us
    unnamed x37, local copies, waits for them, and re-layouts  13.6 us
    pallas_call x1, Pallas kernels, encode(): pl.pallas_call(encode_kernel, out_shape=(jax.ShapeDtypeStruct((4, rows, 5...  10.9 us
    ppermute x1, waiting for transfers between devices, per_device(): b1 = lax.ppermute(pages, 'zl', pair)  10.6 us
    slice x1, local copies, waits for them, and re-layouts, per_device(): keys = cache[:, :, 0, :].reshape(-1, 2, HEAD_DIM)  9.85 us
    ppermute x1, waiting for transfers between devices, per_device(): piece = lax.ppermute(piece, ('zh', 'zl'), cross)  9.77 us
    dynamic_update_slice x4, local copies, waits for them, and re-layouts, per_device(): new_pages = lax.dynamic_update_slice_in_dim(new_pages, got, z_src[i] * 8, 0)  9.39 us
  transfers between devices with their start and end apart: 28, of which 9 were waited for; matrix products, arithmetic and copies ran while one was open for 15% of the time, Pallas kernels for 31%

profile of v1, /device:TPU:2, one launch (start us, length us, event | category | flops | bytes accessed | tf_op | source)
XLA Modules:
  0.0 321.0 jit_solution(11749318039239439997)
XLA Ops:
  1.7 6.4 %collective-permute-start.6 = (bf16[72,1152]{1,0:T(8,128)(2,1)S(1)}, bf16[72,1152]{1,0:T(8,128)(2,1)S(1)}, u32[]{:S(2)}, u32[]{:S(2)}) collective-permute-start(bf16[72,1152]{1,0:T(8,128)(2,1)S(1)} %constant_dynamic-slice_fusion.1), channel_id=1, source_target_pairs={{0,160},{16,176},{32,128},{48,144},{128,32},{144,48},{160,0},{176,... | collective-permute-start | bytes 497672 | tf_op jit(solution)/shard_map/ppermute | solution.py:151
  10.7 9.8 %collective-permute-done.6 = bf16[72,1152]{1,0:T(8,128)(2,1)S(1)} collective-permute-done((bf16[72,1152]{1,0:T(8,128)(2,1)S(1)}, bf16[72,1152]{1,0:T(8,128)(2,1)S(1)}, u32[]{:S(2)}, u32[]{:S(2)}) %collective-permute-start.6) | collective-permute-done | bytes 165920 | tf_op jit(solution)/shard_map/ppermute | solution.py:151
  20.5 1.6 collective-permute-start.7
  22.0 2.9 collective-permute-start.8
  24.9 1.3 collective-permute-start.9
  26.4 1.6 collective-permute-start.1
  28.5 3.3 %collective-permute-done.8 = bf16[72,1152]{1,0:T(8,128)(2,1)S(1)} collective-permute-done((bf16[72,1152]{1,0:T(8,128)(2,1)S(1)}, bf16[72,1152]{1,0:T(8,128)(2,1)S(1)}, u32[]{:S(2)}, u32[]{:S(2)}) %collective-permute-start.8) | collective-permute-done | bytes 165920 | tf_op jit(solution)/shard_map/ppermute | solution.py:155
  32.6 3.2 collective-permute-done.1.x_left
  36.5 1.5 collective-permute-start.3
  39.3 6.5 %copy.82 = bf16[144,8,2,1024]{3,1,2,0:T(8,128)(2,1)} copy(bf16[144,8,2,1024]{3,2,1,0:T(2,128)(2,1)} %bitcast.101) | data formatting | bytes 9437184
  48.6 2.3 copy-done.1
  51.9 10.9 %encode.1 = (bf16[4,512,512]{2,1,0:T(8,128)(2,1)}, f32[8,512]{1,0:T(8,128)S(1)}) custom-call(s32[8]{0:T(128)S(1)} %stack.68.order, bf16[512,288]{1,0:T(8,128)(2,1)S(1)} %copy-done.4, bf16[512,288]{1,0:T(8,128)(2,1)S(1)} %collective-permute-done.1.x_left, bf16[512,288]{1,0:T(8,128)(2,1)S(1)} %collective-permute-done.2.x_right, ...), custom_call_target="tpu_custom_call" | custom-call | tf_op jit(solution)/shard_map/encode/pallas_call | solution.py:81
  62.8 7.5 %all-to-all-start = ((bf16[4,512,512]{2,1,0:T(8,128)(2,1)}), bf16[4,512,512]{2,1,0:T(8,128)(2,1)}, u32[]{:S(2)}, u32[]{:S(2)}) async-start(bf16[4,512,512]{2,1,0:T(8,128)(2,1)} %get-tuple-element.4), calls=%async_computation | async-start | bytes 4194304 | tf_op jit(solution)/shard_map/all_to_all | solution.py:182
  71.0 9.9 %slice_reduce_fusion.1 = (bf16[16,128,256]{2,1,0:T(8,128)(2,1)}, bf16[16,128,256]{2,1,0:T(8,128)(2,1)}) fusion(bf16[16,128,2,256]{3,2,1,0:T(2,128)(2,1)S(1)} %copy-done.5), kind=kLoop, calls=%fused_computation.10 | loop fusion | bytes 4194304 | tf_op jit(solution)/shard_map/slice | solution.py:229
  80.8 1.5 collective-permute-start.11
  82.8 2.1 collective-permute-start.13
  84.9 6.4 %collective-permute-done.11 = f32[8,512]{1,0:T(8,128)S(1)} collective-permute-done((f32[8,512]{1,0:T(8,128)S(1)}, f32[8,512]{1,0:T(8,128)S(1)}, u32[]{:S(2)}, u32[]{:S(2)}) %collective-permute-start.11) | collective-permute-done | bytes 16416 | tf_op jit(solution)/shard_map/ppermute | solution.py:180
  91.3 1.9 collective-permute-done.13
  93.3 2.0 convert_reduce_fusion
  96.3 1.9 pad_maximum_fusion.first.second
  99.0 33.5 %pick.4 = bf16[8,128,2,256]{3,2,1,0:T(2,128)(2,1)} custom-call(s32[8]{0:T(128)} %get-tuple-element.13.code, bf16[4,128,2,256]{3,2,1,0:T(2,128)(2,1)} %pad_maximum_fusion.first.second, bf16[4,128,2,256]{3,2,1,0:T(2,128)(2,1)} %pad_maximum_fusion.first.second, bf16[128,2,256]{2,1,0:T(2,128)(2,1)} %broadcast_in_dim.93.zero), custom_call_target="tpu_custom_call" | custom-call | tf_op jit(solution)/shard_map/pick/pallas_call | solution.py:121
  132.5 6.4 %all-to-all-start.1 = ((bf16[8,128,2,256]{3,2,1,0:T(2,128)(2,1)}), bf16[8,128,2,256]{3,2,1,0:T(2,128)(2,1)S(1)}, u32[]{:S(2)}, u32[]{:S(2)}) async-start(bf16[8,128,2,256]{3,2,1,0:T(2,128)(2,1)} %pick.4), calls=%async_computation.1 | async-start | bytes 2097152 | tf_op jit(solution)/shard_map/all_to_all | solution.py:217
  139.6 1.5 collective-permute-start.15
  141.1 10.6 %collective-permute-done.14.first.second = bf16[4,128,2,256]{3,2,1,0:T(2,128)(2,1)S(1)} collective-permute-done((bf16[4,128,2,256]{3,2,1,0:T(2,128)(2,1)S(1)}, bf16[4,128,2,256]{3,2,1,0:T(2,128)(2,1)S(1)}, u32[]{:S(2)}, u32[]{:S(2)}) %collective-permute-start.14) | collective-permute-done | bytes 524320 | tf_op jit(solution)/shard_map/ppermute | solution.py:209
  152.4 33.5 %pick.5 = bf16[8,128,2,256]{3,2,1,0:T(2,128)(2,1)} custom-call(s32[8]{0:T(128)} %get-tuple-element.12.code, bf16[4,128,2,256]{3,2,1,0:T(2,128)(2,1)} %copy-done.7, bf16[4,128,2,256]{3,2,1,0:T(2,128)(2,1)} %copy-done.7, bf16[128,2,256]{2,1,0:T(2,128)(2,1)} %broadcast_in_dim.93.zero), custom_call_target="tpu_custom_call" | custom-call | tf_op jit(solution)/shard_map/pick/pallas_call | solution.py:121
  186.0 4.5 %all-to-all-start.2 = ((bf16[8,128,2,256]{3,2,1,0:T(2,128)(2,1)}), bf16[8,128,2,256]{3,2,1,0:T(2,128)(2,1)S(1)}, u32[]{:S(2)}, u32[]{:S(2)}) async-start(bf16[8,128,2,256]{3,2,1,0:T(2,128)(2,1)} %pick.5), calls=%async_computation.2 | async-start | bytes 2097152 | tf_op jit(solution)/shard_map/all_to_all | solution.py:217
  190.6 2.1 reshape.311
  193.3 1.3 collective-permute-start.16
  194.6 1.7 fusion.29
  196.3 1.5 collective-permute-start.17
  198.4 2.1 reshape.312
  200.6 1.5 convolution_bitcast_fusion.1
  202.2 4.0 %collective-permute-done.16.second = bf16[4,128,2,256]{3,2,1,0:T(2,128)(2,1)S(1)} collective-permute-done((bf16[4,128,2,256]{3,2,1,0:T(2,128)(2,1)}, bf16[4,128,2,256]{3,2,1,0:T(2,128)(2,1)S(1)}, u32[]{:S(2)}, u32[]{:S(2)}) %collective-permute-start.16) | collective-permute-done | bytes 524320 | tf_op jit(solution)/shard_map/ppermute | solution.py:212
  207.0 33.5 %pick.6 = bf16[8,128,2,256]{3,2,1,0:T(2,128)(2,1)} custom-call(s32[8]{0:T(128)} %get-tuple-element.11.code, bf16[4,128,2,256]{3,2,1,0:T(2,128)(2,1)} %collective-permute-done.15.first, bf16[4,128,2,256]{3,2,1,0:T(2,128)(2,1)} %copy-done.9, bf16[128,2,256]{2,1,0:T(2,128)(2,1)} %broadcast_in_dim.93.zero), custom_call_target="tpu_custom_call" | custom-call | tf_op jit(solution)/shard_map/pick/pallas_call | solution.py:121
  240.6 4.5 %all-to-all-start.3 = ((bf16[8,128,2,256]{3,2,1,0:T(2,128)(2,1)}), bf16[8,128,2,256]{3,2,1,0:T(2,128)(2,1)}, u32[]{:S(2)}, u32[]{:S(2)}) async-start(bf16[8,128,2,256]{3,2,1,0:T(2,128)(2,1)} %pick.6), calls=%async_computation.3 | async-start | bytes 2097152 | tf_op jit(solution)/shard_map/all_to_all | solution.py:217
  245.5 1.3 collective-permute-start.18
  247.3 2.0 collective-permute-start.19
  249.4 6.1 %collective-permute-done.19 = f32[32,128]{1,0:T(8,128)S(1)} collective-permute-done((f32[32,128]{1,0:T(8,128)S(1)}, f32[32,128]{1,0:T(8,128)S(1)}, u32[]{:S(2)}, u32[]{:S(2)}) %collective-permute-start.19) | collective-permute-done | bytes 16416 | tf_op jit(solution)/shard_map/ppermute | solution.py:242
  255.5 2.7 collective-permute-start.20
  258.2 2.6 collective-permute-done.20
  262.1 33.5 %pick.7 = bf16[8,128,2,256]{3,2,1,0:T(2,128)(2,1)} custom-call(s32[8]{0:T(128)} %get-tuple-element.10.code, bf16[4,128,2,256]{3,2,1,0:T(2,128)(2,1)} %collective-permute-done.17.first, bf16[4,128,2,256]{3,2,1,0:T(2,128)(2,1)} %copy-done.8, bf16[128,2,256]{2,1,0:T(2,128)(2,1)} %broadcast_in_dim.93.zero), custom_call_target="tpu_custom_call" | custom-call | tf_op jit(solution)/shard_map/pick/pallas_call | solution.py:121
  295.6 4.3 %all-to-all-start.4 = ((bf16[8,128,2,256]{3,2,1,0:T(2,128)(2,1)}), bf16[8,128,2,256]{3,2,1,0:T(2,128)(2,1)}, u32[]{:S(2)}, u32[]{:S(2)}) async-start(bf16[8,128,2,256]{3,2,1,0:T(2,128)(2,1)} %pick.7), calls=%async_computation.4 | async-start | bytes 2097152 | tf_op jit(solution)/shard_map/all_to_all | solution.py:217
  300.0 2.1 collective-permute-start.22
  305.8 5.8 %broadcast_in_dim.85 = bf16[32,128,2,256]{3,2,1,0:T(2,128)(2,1)} broadcast(bf16[]{:T(256)} %constant.162.clone.1), dimensions={} | broadcast | bytes 4194306 | tf_op jit(solution)/shard_map/broadcast_in_dim | solution.py:214
  311.6 1.8 constant_dynamic-update-slice_fusion.3
  313.4 1.8 constant_dynamic-update-slice_fusion.2
  315.2 2.9 constant_dynamic-update-slice_fusion.1
  318.1 2.9 constant_dynamic-update-slice_fusion
  (125 shorter events, 20.9 us)
Async XLA Ops:
  0.6 194.0 %copy-start = (bf16[4,512]{1,0:T(4,128)(2,1)S(1)}, bf16[4,512]{1,0:T(4,128)(2,1)}, u32[]{:S(2)}) copy-start(bf16[4,512]{1,0:T(4,128)(2,1)} %param.21) | copy-start | bytes 12292
  0.6 47.9 %collective-permute-start.5 = (bf16[288,1152]{1,0:T(8,128)(2,1)}, bf16[288,1152]{1,0:T(8,128)(2,1)S(1)}, u32[]{:S(2)}, u32[]{:S(2)}) collective-permute-start(bf16[288,1152]{1,0:T(8,128)(2,1)} %w_own.1), channel_id=1, source_target_pairs={{0,64},{64,0},{1,65},{65,1},{2,66},{66,2},{3,67},{67,3},{4,68},{68... | collective-permute-start | bytes 1990664 | tf_op jit(solution)/shard_map/ppermute | solution.py:147
  1.7 18.8 %collective-permute-start.6 = (bf16[72,1152]{1,0:T(8,128)(2,1)S(1)}, bf16[72,1152]{1,0:T(8,128)(2,1)S(1)}, u32[]{:S(2)}, u32[]{:S(2)}) collective-permute-start(bf16[72,1152]{1,0:T(8,128)(2,1)S(1)} %constant_dynamic-slice_fusion.1), channel_id=1, source_target_pairs={{0,160},{16,176},{32,128},{48,144},{128,32},{144,48},{160,0},{176,... | collective-permute-start | bytes 497672 | tf_op jit(solution)/shard_map/ppermute | solution.py:151
  9.3 17.1 %collective-permute-start = (bf16[512,288]{1,0:T(8,128)(2,1)S(1)}, bf16[512,288]{1,0:T(8,128)(2,1)S(1)}, u32[]{:S(2)}, u32[]{:S(2)}) collective-permute-start(bf16[512,288]{1,0:T(8,128)(2,1)S(1)} %copy.51), channel_id=1, source_target_pairs={{0,64},{64,160},{16,80},{80,176},{32,96},{96,128},{48,112},{112,14... | collective-permute-start | bytes 884744 | tf_op jit(solution)/shard_map/ppermute | solution.py:144
  20.5 7.5 %collective-permute-start.7 = (bf16[72,1152]{1,0:T(8,128)(2,1)S(1)}, bf16[72,1152]{1,0:T(8,128)(2,1)S(1)}, u32[]{:S(2)}, u32[]{:S(2)}) collective-permute-start(bf16[72,1152]{1,0:T(8,128)(2,1)S(1)} %collective-permute-done.6), channel_id=1, source_target_pairs={{0,4},{4,8},{8,12},{12,0},{1,5},{5,9},{9,13},{13,1},{2,6},{6,10},{... | collective-permute-start | bytes 497672 | tf_op jit(solution)/shard_map/ppermute | solution.py:153
  22.0 9.7 %collective-permute-start.8 = (bf16[72,1152]{1,0:T(8,128)(2,1)S(1)}, bf16[72,1152]{1,0:T(8,128)(2,1)S(1)}, u32[]{:S(2)}, u32[]{:S(2)}) collective-permute-start(bf16[72,1152]{1,0:T(8,128)(2,1)S(1)} %collective-permute-done.6), channel_id=1, source_target_pairs={{0,8},{4,12},{8,0},{12,4},{1,9},{5,13},{9,1},{13,5},{2,10},{6,14},... | collective-permute-start | bytes 497672 | tf_op jit(solution)/shard_map/ppermute | solution.py:155
  24.9 6.9 %collective-permute-start.9 = (bf16[72,1152]{1,0:T(8,128)(2,1)S(1)}, bf16[72,1152]{1,0:T(8,128)(2,1)S(1)}, u32[]{:S(2)}, u32[]{:S(2)}) collective-permute-start(bf16[72,1152]{1,0:T(8,128)(2,1)S(1)} %collective-permute-done.6), channel_id=1, source_target_pairs={{0,12},{4,0},{8,4},{12,8},{1,13},{5,1},{9,5},{13,9},{2,14},{6,2},{... | collective-permute-start | bytes 497672 | tf_op jit(solution)/shard_map/ppermute | solution.py:154
  26.4 12.9 %copy-start.3 = (bf16[512,288]{1,0:T(8,128)(2,1)}, bf16[512,288]{1,0:T(8,128)(2,1)S(1)}, u32[]{:S(2)}) copy-start(bf16[512,288]{1,0:T(8,128)(2,1)S(1)} %collective-permute-done.x_own) | copy-start | bytes 884740
  26.4 9.4 %collective-permute-start.1 = (bf16[512,288]{1,0:T(8,128)(2,1)S(1)}, bf16[512,288]{1,0:T(8,128)(2,1)S(1)}, u32[]{:S(2)}, u32[]{:S(2)}) collective-permute-start(bf16[512,288]{1,0:T(8,128)(2,1)S(1)} %collective-permute-done.x_own), channel_id=1, source_target_pairs={{0,1},{1,2},{2,3},{3,0},{4,5},{5,6},{6,7},{7,4},{8,9},{9,10},{10,1... | collective-permute-start | bytes 884744 | tf_op jit(solution)/shard_map/ppermute | solution.py:163
  28.0 10.1 %collective-permute-start.2 = (bf16[512,288]{1,0:T(8,128)(2,1)S(1)}, bf16[512,288]{1,0:T(8,128)(2,1)S(1)}, u32[]{:S(2)}, u32[]{:S(2)}) collective-permute-start(bf16[512,288]{1,0:T(8,128)(2,1)S(1)} %collective-permute-done.x_own), channel_id=1, source_target_pairs={{0,3},{1,0},{2,1},{3,2},{4,7},{5,4},{6,5},{7,6},{8,11},{9,8},{10,9... | collective-permute-start | bytes 884744 | tf_op jit(solution)/shard_map/ppermute | solution.py:164
  31.9 16.7 %collective-permute-start.10 = (bf16[288,1152]{1,0:T(8,128)(2,1)S(1)}, bf16[288,1152]{1,0:T(8,128)(2,1)S(1)}, u32[]{:S(2)}, u32[]{:S(2)}) collective-permute-start(bf16[288,1152]{1,0:T(8,128)(2,1)S(1)} %bitcast.99), channel_id=1, source_target_pairs={{0,64},{64,0},{1,65},{65,1},{2,66},{66,2},{3,67},{67,3},{4,68},{68... | collective-permute-start | bytes 1990664 | tf_op jit(solution)/shard_map/ppermute | solution.py:160
  36.5 10.9 %collective-permute-start.3 = (bf16[256,288]{1,0:T(8,128)(2,1)}, bf16[256,288]{1,0:T(8,128)(2,1)}, u32[]{:S(2)}, u32[]{:S(2)}) collective-permute-start(bf16[256,288]{1,0:T(8,128)(2,1)} %slice.74), channel_id=1, source_target_pairs={{0,1},{1,2},{2,3},{3,0},{4,5},{5,6},{6,7},{7,4},{8,9},{9,10},{10,1... | collective-permute-start | bytes 442376 | tf_op jit(solution)/shard_map/ppermute | solution.py:165
  38.7 8.7 %collective-permute-start.4 = (bf16[256,288]{1,0:T(8,128)(2,1)}, bf16[256,288]{1,0:T(8,128)(2,1)}, u32[]{:S(2)}, u32[]{:S(2)}) collective-permute-start(bf16[256,288]{1,0:T(8,128)(2,1)} %slice.75), channel_id=1, source_target_pairs={{0,3},{1,0},{2,1},{3,2},{4,7},{5,4},{6,5},{7,6},{8,11},{9,8},{10,9... | collective-permute-start | bytes 442376 | tf_op jit(solution)/shard_map/ppermute | solution.py:166
  39.3 6.5 %copy-start.10 = (f32[1152]{0:T(1024)S(1)}, f32[1152]{0:T(1024)}, u32[]{:S(2)}) copy-start(f32[1152]{0:T(1024)} %param.15) | copy-start | bytes 13828
  39.3 6.6 %copy-start.11 = (f32[1152]{0:T(1024)S(1)}, f32[1152]{0:T(1024)}, u32[]{:S(2)}) copy-start(f32[1152]{0:T(1024)} %param.16) | copy-start | bytes 13828
  39.3 6.7 %copy-start.12 = (f32[1152]{0:T(1024)S(1)}, f32[1152]{0:T(1024)}, u32[]{:S(2)}) copy-start(f32[1152]{0:T(1024)} %param.18) | copy-start | bytes 13828
  39.3 6.7 %copy-start.13 = (f32[1152]{0:T(1024)S(1)}, f32[1152]{0:T(1024)}, u32[]{:S(2)}) copy-start(f32[1152]{0:T(1024)} %param.19) | copy-start | bytes 13828
  39.3 9.2 %copy-start.2 = (bf16[288,1152]{1,0:T(8,128)(2,1)S(1)}, bf16[288,1152]{1,0:T(8,128)(2,1)}, u32[]{:S(2)}) copy-start(bf16[288,1152]{1,0:T(8,128)(2,1)} %w_own.1) | copy-start | bytes 1990660
  48.6 2.3 copy-start.1
  50.9 1.0 copy-start.4
  62.8 8.2 %copy-start.5 = (bf16[16,128,2,256]{3,2,1,0:T(2,128)(2,1)S(1)}, bf16[16,128,2,256]{3,2,1,0:T(2,128)(2,1)}, u32[]{:S(2)}) copy-start(bf16[16,128,2,256]{3,2,1,0:T(2,128)(2,1)} %param.22) | copy-start | bytes 6291460
  62.8 30.5 %all-to-all-start = ((bf16[4,512,512]{2,1,0:T(8,128)(2,1)}), bf16[4,512,512]{2,1,0:T(8,128)(2,1)}, u32[]{:S(2)}, u32[]{:S(2)}) async-start(bf16[4,512,512]{2,1,0:T(8,128)(2,1)} %get-tuple-element.4), calls=%async_computation | async-start | bytes 4194304 | tf_op jit(solution)/shard_map/all_to_all | solution.py:182
  70.3 14.6 %copy-start.14 = (s32[1,4]{1,0:T(1,128)S(1)}, s32[1,4]{1,0:T(1,128)}, u32[]{:S(2)}) copy-start(s32[1,4]{1,0:T(1,128)} %param.23) | copy-start | bytes 52
  80.8 10.5 %collective-permute-start.11 = (f32[8,512]{1,0:T(8,128)S(1)}, f32[8,512]{1,0:T(8,128)S(1)}, u32[]{:S(2)}, u32[]{:S(2)}) collective-permute-start(f32[8,512]{1,0:T(8,128)S(1)} %get-tuple-element.5), channel_id=1, source_target_pairs={{0,1},{1,2},{2,3},{3,0},{4,5},{5,6},{6,7},{7,4},{8,9},{9,10},{10,1... | collective-permute-start | bytes 49160 | tf_op jit(solution)/shard_map/ppermute | solution.py:180
  82.3 9.0 %collective-permute-start.12 = (f32[8,512]{1,0:T(8,128)S(1)}, f32[8,512]{1,0:T(8,128)S(1)}, u32[]{:S(2)}, u32[]{:S(2)}) collective-permute-start(f32[8,512]{1,0:T(8,128)S(1)} %get-tuple-element.5), channel_id=1, source_target_pairs={{0,3},{1,0},{2,1},{3,2},{4,7},{5,4},{6,5},{7,6},{8,11},{9,8},{10,9... | collective-permute-start | bytes 49160 | tf_op jit(solution)/shard_map/ppermute | solution.py:180
  82.8 10.4 %collective-permute-start.13 = (f32[8,512]{1,0:T(8,128)S(1)}, f32[8,512]{1,0:T(8,128)S(1)}, u32[]{:S(2)}, u32[]{:S(2)}) collective-permute-start(f32[8,512]{1,0:T(8,128)S(1)} %get-tuple-element.5), channel_id=1, source_target_pairs={{0,2},{1,3},{2,0},{3,1},{4,6},{5,7},{6,4},{7,5},{8,10},{9,11},{10,... | collective-permute-start | bytes 49160 | tf_op jit(solution)/shard_map/ppermute | solution.py:180
  95.5 44.0 %copy-start.15 = (s32[1,16]{1,0:T(1,128)S(1)}, s32[1,16]{1,0:T(1,128)}, u32[]{:S(2)}) copy-start(s32[1,16]{1,0:T(1,128)} %param.24) | copy-start | bytes 196
  98.2 40.9 %copy-start.6 = (bf16[4,128,2,256]{3,2,1,0:T(2,128)(2,1)S(1)}, bf16[4,128,2,256]{3,2,1,0:T(2,128)(2,1)}, u32[]{:S(2)}) copy-start(bf16[4,128,2,256]{3,2,1,0:T(2,128)(2,1)} %pad_maximum_fusion.first.second) | copy-start | bytes 1572868
  132.5 60.2 %copy-start.16 = (s32[1,2]{1,0:T(1,128)S(1)}, s32[1,2]{1,0:T(1,128)}, u32[]{:S(2)}) copy-start(s32[1,2]{1,0:T(1,128)} %param.26) | copy-start | bytes 28
  132.5 53.5 %all-to-all-start.1 = ((bf16[8,128,2,256]{3,2,1,0:T(2,128)(2,1)}), bf16[8,128,2,256]{3,2,1,0:T(2,128)(2,1)S(1)}, u32[]{:S(2)}, u32[]{:S(2)}) async-start(bf16[8,128,2,256]{3,2,1,0:T(2,128)(2,1)} %pick.4), calls=%async_computation.1 | async-start | bytes 2097152 | tf_op jit(solution)/shard_map/all_to_all | solution.py:217
  139.1 12.5 %collective-permute-start.14 = (bf16[4,128,2,256]{3,2,1,0:T(2,128)(2,1)S(1)}, bf16[4,128,2,256]{3,2,1,0:T(2,128)(2,1)S(1)}, u32[]{:S(2)}, u32[]{:S(2)}) collective-permute-start(bf16[4,128,2,256]{3,2,1,0:T(2,128)(2,1)S(1)} %copy-done.6), channel_id=1, source_target_pairs={{0,16},{16,0},{32,48},{48,32},{1,17},{17,1},{33,49},{49,33},{2,18}... | collective-permute-start | bytes 1572872 | tf_op jit(solution)/shard_map/ppermute | solution.py:209
  139.6 53.7 %collective-permute-start.15 = (bf16[4,128,2,256]{3,2,1,0:T(2,128)(2,1)S(1)}, bf16[4,128,2,256]{3,2,1,0:T(2,128)(2,1)}, u32[]{:S(2)}, u32[]{:S(2)}) collective-permute-start(bf16[4,128,2,256]{3,2,1,0:T(2,128)(2,1)S(1)} %copy-done.6), channel_id=1, source_target_pairs={{16,32},{32,16},{17,33},{33,17},{18,34},{34,18},{19,35},{35,19},{2... | collective-permute-start | bytes 1572872 | tf_op jit(solution)/shard_map/ppermute | solution.py:210
  151.6 0.8 copy-start.7
  186.0 54.6 %all-to-all-start.2 = ((bf16[8,128,2,256]{3,2,1,0:T(2,128)(2,1)}), bf16[8,128,2,256]{3,2,1,0:T(2,128)(2,1)S(1)}, u32[]{:S(2)}, u32[]{:S(2)}) async-start(bf16[8,128,2,256]{3,2,1,0:T(2,128)(2,1)} %pick.5), calls=%async_computation.2 | async-start | bytes 2097152 | tf_op jit(solution)/shard_map/all_to_all | solution.py:217
  193.3 12.9 %collective-permute-start.16 = (bf16[4,128,2,256]{3,2,1,0:T(2,128)(2,1)}, bf16[4,128,2,256]{3,2,1,0:T(2,128)(2,1)S(1)}, u32[]{:S(2)}, u32[]{:S(2)}) collective-permute-start(bf16[4,128,2,256]{3,2,1,0:T(2,128)(2,1)} %collective-permute-done.15.first), channel_id=1, source_target_pairs={{16,0},{32,48},{17,1},{33,49},{18,2},{34,50},{19,3},{35,51},{20,4}... | collective-permute-start | bytes 1572872 | tf_op jit(solution)/shard_map/ppermute | solution.py:212
  196.3 49.2 %collective-permute-start.17 = (bf16[4,128,2,256]{3,2,1,0:T(2,128)(2,1)}, bf16[4,128,2,256]{3,2,1,0:T(2,128)(2,1)}, u32[]{:S(2)}, u32[]{:S(2)}) collective-permute-start(bf16[4,128,2,256]{3,2,1,0:T(2,128)(2,1)} %copy-done.7), channel_id=1, source_target_pairs={{16,32},{32,16},{17,33},{33,17},{18,34},{34,18},{19,35},{35,19},{2... | collective-permute-start | bytes 1572872 | tf_op jit(solution)/shard_map/ppermute | solution.py:211
  206.2 0.8 copy-start.9
  240.6 55.1 %all-to-all-start.3 = ((bf16[8,128,2,256]{3,2,1,0:T(2,128)(2,1)}), bf16[8,128,2,256]{3,2,1,0:T(2,128)(2,1)}, u32[]{:S(2)}, u32[]{:S(2)}) async-start(bf16[8,128,2,256]{3,2,1,0:T(2,128)(2,1)} %pick.6), calls=%async_computation.3 | async-start | bytes 2097152 | tf_op jit(solution)/shard_map/all_to_all | solution.py:217
  245.5 15.8 %collective-permute-start.18 = (bf16[4,128,2,256]{3,2,1,0:T(2,128)(2,1)}, bf16[4,128,2,256]{3,2,1,0:T(2,128)(2,1)S(1)}, u32[]{:S(2)}, u32[]{:S(2)}) collective-permute-start(bf16[4,128,2,256]{3,2,1,0:T(2,128)(2,1)} %collective-permute-done.17.first), channel_id=1, source_target_pairs={{16,0},{32,48},{17,1},{33,49},{18,2},{34,50},{19,3},{35,51},{20,4}... | collective-permute-start | bytes 1572872 | tf_op jit(solution)/shard_map/ppermute | solution.py:213
  247.3 8.1 %collective-permute-start.19 = (f32[32,128]{1,0:T(8,128)S(1)}, f32[32,128]{1,0:T(8,128)S(1)}, u32[]{:S(2)}, u32[]{:S(2)}) collective-permute-start(f32[32,128]{1,0:T(8,128)S(1)} %pad_maximum_fusion.2), channel_id=1, source_target_pairs={{0,4},{4,0},{8,12},{12,8},{1,5},{5,1},{9,13},{13,9},{2,6},{6,2},{1... | collective-permute-start | bytes 49160 | tf_op jit(solution)/shard_map/ppermute | solution.py:242
  255.5 5.2 %collective-permute-start.20 = (f32[32,128]{1,0:T(8,128)S(1)}, f32[32,128]{1,0:T(8,128)S(1)}, u32[]{:S(2)}, u32[]{:S(2)}) collective-permute-start(f32[32,128]{1,0:T(8,128)S(1)} %fusion.26), channel_id=1, source_target_pairs={{0,8},{4,12},{8,0},{12,4},{1,9},{5,13},{9,1},{13,5},{2,10},{6,14},... | collective-permute-start | bytes 49160 | tf_op jit(solution)/shard_map/ppermute | solution.py:242
  260.8 39.2 %collective-permute-start.21 = (f32[32,128]{1,0:T(8,128)S(1)}, f32[32,128]{1,0:T(8,128)S(1)}, u32[]{:S(2)}, u32[]{:S(2)}) collective-permute-start(f32[32,128]{1,0:T(8,128)S(1)} %add.247), channel_id=1, source_target_pairs={{0,16},{16,0},{32,48},{48,32},{1,17},{17,1},{33,49},{49,33},{2,18}... | collective-permute-start | bytes 49160 | tf_op jit(solution)/shard_map/ppermute | solution.py:242
  261.3 0.8 copy-start.8
  295.6 22.5 %all-to-all-start.4 = ((bf16[8,128,2,256]{3,2,1,0:T(2,128)(2,1)}), bf16[8,128,2,256]{3,2,1,0:T(2,128)(2,1)}, u32[]{:S(2)}, u32[]{:S(2)}) async-start(bf16[8,128,2,256]{3,2,1,0:T(2,128)(2,1)} %pick.7), calls=%async_computation.4 | async-start | bytes 2097152 | tf_op jit(solution)/shard_map/all_to_all | solution.py:217
  300.0 5.2 %collective-permute-start.22 = (f32[32,128]{1,0:T(8,128)S(1)}, f32[32,128]{1,0:T(8,128)S(1)}, u32[]{:S(2)}, u32[]{:S(2)}) collective-permute-start(f32[32,128]{1,0:T(8,128)S(1)} %add.248), channel_id=1, source_target_pairs={{0,32},{16,48},{32,0},{48,16},{1,33},{17,49},{33,1},{49,17},{2,34}... | collective-permute-start | bytes 49160 | tf_op jit(solution)/shard_map/ppermute | solution.py:242

commit v2 on v1

--- a/solution.py
+++ b/solution.py
@@ -117,15 +117,37 @@
 
 
 def pick(code, first, second, zero):
-    any_spec = pl.BlockSpec(memory_space=pl.ANY)
+    vmem = pl.BlockSpec(memory_space=pltpu.VMEM)
     return pl.pallas_call(
         pick_kernel,
         out_shape=jax.ShapeDtypeStruct((8,) + first.shape[1:], first.dtype),
-        in_specs=[pl.BlockSpec(memory_space=pltpu.SMEM), any_spec, any_spec, any_spec],
-        out_specs=any_spec,
+        in_specs=[pl.BlockSpec(memory_space=pltpu.SMEM), vmem, vmem, vmem],
+        out_specs=pl.BlockSpec(memory_space=pl.ANY),
         scratch_shapes=[pltpu.SemaphoreType.DMA],
         name="pick",
     )(code, first, second, zero)
+
+
+def place_kernel(where, got, *refs):
+    out, sem = refs[-2:]
+    copy = pltpu.make_async_copy(got, out.at[pl.ds(where[0] * 8, 8)], sem)
+    copy.start()
+    copy.wait()
+
+
+def place(where, got, buffer):
+    any_spec = pl.BlockSpec(memory_space=pl.ANY)
+    vmem = pl.BlockSpec(memory_space=pltpu.VMEM)
+    given = (where, got) if buffer is None else (where, got, buffer)
+    return pl.pallas_call(
+        place_kernel,
+        out_shape=jax.ShapeDtypeStruct((32,) + got.shape[1:], got.dtype),
+        in_specs=[pl.BlockSpec(memory_space=pltpu.SMEM), vmem] + [any_spec] * (len(given) - 2),
+        out_specs=any_spec,
+        scratch_shapes=[pltpu.SemaphoreType.DMA],
+        input_output_aliases={} if buffer is None else {2: 0},
+        name="place",
+    )(*given)
 
 
 def per_device(
@@ -211,11 +233,11 @@
     b3m = lax.ppermute(b1, "zl", mid)
     b2o = lax.ppermute(b2m, "zl", outer)
     b3o = lax.ppermute(b3m, "zl", outer)
-    new_pages = jnp.zeros((32, PAGE, 2, 256), jnp.bfloat16)
+    new_pages = None
     for i, (f, s) in enumerate(((pages, pages), (b1, b1), (b2m, b2o), (b3m, b3o))):
         sent = pick(code[i], f, s, zero)
         got = lax.all_to_all(sent, "y", 0, 0, tiled=True)
-        new_pages = lax.dynamic_update_slice_in_dim(new_pages, got, z_src[i] * 8, 0)
+        new_pages = place(z_src[i : i + 1].astype(jnp.int32), got, new_pages)
 
     req_count = queries.shape[0]
     query_grid = queries.reshape(req_count, 2, 2, HEAD_DIM)

time: 323 us -> 208 us (0.64)
  Pallas kernels: 145 us -> 31.1 us
  waiting for transfers between devices: 47.8 us -> 67.1 us
  local copies, waits for them, and re-layouts: 52.2 us -> 36.8 us
    pallas_call x4, Pallas kernels: 134 us -> 8.88 us  [pick(): pl.pallas_call(pick_kernel, out_shape=jax.ShapeDtypeStruct((8,) + first.s...]
    pallas_call x0 -> x4, Pallas kernels: none -> 11.4 us  [place(): pl.pallas_call(place_kernel, out_shape=jax.ShapeDtypeStruct((32,) + got.s...]
    dynamic_update_slice x4 -> x0, local copies, waits for them, and re-layouts: 9.39 us -> none  [per_device(): new_pages = lax.dynamic_update_slice_in_dim(new_pages, got, z_src[i] * 8, 0)]
    ppermute x4, waiting for transfers between devices: 8.65 us -> 17.4 us  [per_device(): both = both + lax.ppermute(both, axis, [(i, i ^ m) for i in range(4)])]
    ppermute x1, waiting for transfers between devices: 0.01 us -> 8.52 us  [per_device(): b3o = lax.ppermute(b3m, 'zl', outer)]
    broadcast_in_dim x1 -> x0, local copies, waits for them, and re-layouts: 5.79 us -> none  [per_device(): new_pages = jnp.zeros((32, PAGE, 2, 256), jnp.bfloat16)]
    unnamed x37 -> x47, local copies, waits for them, and re-layouts: 13.6 us -> 14.6 us
  transfers between devices with their start and end apart: 28 -> 28, of which waited for: 9 -> 12; matrix products, arithmetic and copies ran while one was open for 15% -> 17% of each run, Pallas kernels for 31% -> 7%
where the time goes in v2:
time: 208 us; the launch traced here: 207 us
  waiting for transfers between devices  67.1 us (32%)
  starting transfers between devices  59.4 us (29%)
  local copies, waits for them, and re-layouts  36.8 us (18%)
  Pallas kernels  31.1 us (15%)
  other arithmetic  7.35 us (4%)
  matrix products  3.62 us (2%)
    all_to_all x4, starting transfers between devices, per_device(): got = lax.all_to_all(sent, 'y', 0, 0, tiled=True)  20 us
    ppermute x4, waiting for transfers between devices, per_device(): both = both + lax.ppermute(both, axis, [(i, i ^ m) for i in range(4)])  17.4 us
    unnamed x47, local copies, waits for them, and re-layouts  14.6 us
    pallas_call x4, Pallas kernels, place(): pl.pallas_call(place_kernel, out_shape=jax.ShapeDtypeStruct((32,) + got.s...  11.4 us
    pallas_call x1, Pallas kernels, encode(): pl.pallas_call(encode_kernel, out_shape=(jax.ShapeDtypeStruct((4, rows, 5...  10.9 us
    ppermute x1, waiting for transfers between devices, per_device(): b1 = lax.ppermute(pages, 'zl', pair)  10.5 us
    ppermute x1, waiting for transfers between devices, per_device(): piece = lax.ppermute(piece, ('zh', 'zl'), cross)  9.77 us
    slice x1, local copies, waits for them, and re-layouts, per_device(): keys = cache[:, :, 0, :].reshape(-1, 2, HEAD_DIM)  9.51 us
  transfers between devices with their start and end apart: 28, of which 12 were waited for; matrix products, arithmetic and copies ran while one was open for 17% of the time, Pallas kernels for 7%

profile of v2, /device:TPU:2, one launch (start us, length us, event | category | flops | bytes accessed | tf_op | source)
XLA Modules:
  0.0 206.9 jit_solution(8846386326664548462)
XLA Ops:
  1.7 6.4 %collective-permute-start.6 = (bf16[72,1152]{1,0:T(8,128)(2,1)S(1)}, bf16[72,1152]{1,0:T(8,128)(2,1)S(1)}, u32[]{:S(2)}, u32[]{:S(2)}) collective-permute-start(bf16[72,1152]{1,0:T(8,128)(2,1)S(1)} %constant_dynamic-slice_fusion.1), channel_id=1, source_target_pairs={{0,160},{16,176},{32,128},{48,144},{128,32},{144,48},{160,0},{176,... | collective-permute-start | bytes 497672 | tf_op jit(solution)/shard_map/ppermute | solution.py:173
  10.7 9.8 %collective-permute-done.6 = bf16[72,1152]{1,0:T(8,128)(2,1)S(1)} collective-permute-done((bf16[72,1152]{1,0:T(8,128)(2,1)S(1)}, bf16[72,1152]{1,0:T(8,128)(2,1)S(1)}, u32[]{:S(2)}, u32[]{:S(2)}) %collective-permute-start.6) | collective-permute-done | bytes 165920 | tf_op jit(solution)/shard_map/ppermute | solution.py:173
  20.5 1.6 collective-permute-start.7
  22.0 2.9 %collective-permute-start.8 = (bf16[72,1152]{1,0:T(8,128)(2,1)S(1)}, bf16[72,1152]{1,0:T(8,128)(2,1)S(1)}, u32[]{:S(2)}, u32[]{:S(2)}) collective-permute-start(bf16[72,1152]{1,0:T(8,128)(2,1)S(1)} %collective-permute-done.6), channel_id=1, source_target_pairs={{0,8},{4,12},{8,0},{12,4},{1,9},{5,13},{9,1},{13,5},{2,10},{6,14},... | collective-permute-start | bytes 497672 | tf_op jit(solution)/shard_map/ppermute | solution.py:177
  24.9 1.3 collective-permute-start.9
  26.4 1.6 collective-permute-start.1
  28.5 3.3 %collective-permute-done.8 = bf16[72,1152]{1,0:T(8,128)(2,1)S(1)} collective-permute-done((bf16[72,1152]{1,0:T(8,128)(2,1)S(1)}, bf16[72,1152]{1,0:T(8,128)(2,1)S(1)}, u32[]{:S(2)}, u32[]{:S(2)}) %collective-permute-start.8) | collective-permute-done | bytes 165920 | tf_op jit(solution)/shard_map/ppermute | solution.py:177
  32.6 3.2 %collective-permute-done.1.x_left = bf16[512,288]{1,0:T(8,128)(2,1)S(1)} collective-permute-done((bf16[512,288]{1,0:T(8,128)(2,1)S(1)}, bf16[512,288]{1,0:T(8,128)(2,1)S(1)}, u32[]{:S(2)}, u32[]{:S(2)}) %collective-permute-start.1) | collective-permute-done | bytes 294944 | tf_op jit(solution)/shard_map/ppermute | solution.py:185
  36.5 1.5 collective-permute-start.3
  39.3 6.5 %copy.85 = bf16[144,8,2,1024]{3,1,2,0:T(8,128)(2,1)} copy(bf16[144,8,2,1024]{3,2,1,0:T(2,128)(2,1)} %bitcast.97) | data formatting | bytes 9437184
  48.6 2.3 %copy-done.1 = bf16[144,8,2,1024]{3,1,2,0:T(8,128)(2,1)S(1)} copy-done((bf16[144,8,2,1024]{3,1,2,0:T(8,128)(2,1)S(1)}, bf16[144,8,2,1024]{3,1,2,0:T(8,128)(2,1)}, u32[]{:S(2)}) %copy-start.1) | copy-done | bytes 4718616
  51.9 10.9 %encode.1 = (bf16[4,512,512]{2,1,0:T(8,128)(2,1)}, f32[8,512]{1,0:T(8,128)S(1)}) custom-call(s32[8]{0:T(128)S(1)} %stack.73.order, bf16[512,288]{1,0:T(8,128)(2,1)S(1)} %copy-done.4, bf16[512,288]{1,0:T(8,128)(2,1)S(1)} %collective-permute-done.1.x_left, bf16[512,288]{1,0:T(8,128)(2,1)S(1)} %collective-permute-done.2.x_right, ...), custom_call_target="tpu_custom_call" | custom-call | tf_op jit(solution)/shard_map/encode/pallas_call | solution.py:81
  62.8 7.5 %all-to-all-start = ((bf16[4,512,512]{2,1,0:T(8,128)(2,1)}), bf16[4,512,512]{2,1,0:T(8,128)(2,1)}, u32[]{:S(2)}, u32[]{:S(2)}) async-start(bf16[4,512,512]{2,1,0:T(8,128)(2,1)} %get-tuple-element.4), calls=%async_computation | async-start | bytes 4194304 | tf_op jit(solution)/shard_map/all_to_all | solution.py:204
  70.9 9.5 %slice_reduce_fusion.1 = (bf16[16,128,256]{2,1,0:T(8,128)(2,1)}, bf16[16,128,256]{2,1,0:T(8,128)(2,1)S(1)}) fusion(bf16[16,128,2,256]{3,2,1,0:T(2,128)(2,1)S(1)} %copy-done.5), kind=kLoop, calls=%fused_computation.10 | loop fusion | bytes 4194304 | tf_op jit(solution)/shard_map/slice | solution.py:251
  80.5 1.5 collective-permute-start.11
  82.5 2.1 %collective-permute-start.13 = (f32[8,512]{1,0:T(8,128)S(1)}, f32[8,512]{1,0:T(8,128)S(1)}, u32[]{:S(2)}, u32[]{:S(2)}) collective-permute-start(f32[8,512]{1,0:T(8,128)S(1)} %get-tuple-element.5), channel_id=1, source_target_pairs={{0,2},{1,3},{2,0},{3,1},{4,6},{5,7},{6,4},{7,5},{8,10},{9,11},{10,... | collective-permute-start | bytes 49160 | tf_op jit(solution)/shard_map/ppermute | solution.py:202
  84.7 6.6 %collective-permute-done.11 = f32[8,512]{1,0:T(8,128)S(1)} collective-permute-done((f32[8,512]{1,0:T(8,128)S(1)}, f32[8,512]{1,0:T(8,128)S(1)}, u32[]{:S(2)}, u32[]{:S(2)}) %collective-permute-start.11) | collective-permute-done | bytes 16416 | tf_op jit(solution)/shard_map/ppermute | solution.py:202
  91.3 1.9 collective-permute-done.13
  93.3 2.0 convert_reduce_fusion
  96.3 1.9 pad_maximum_fusion.first.second
  99.0 2.3 %pick.7 = bf16[8,128,2,256]{3,2,1,0:T(2,128)(2,1)} custom-call(s32[8]{0:T(128)} %get-tuple-element.10.code, bf16[4,128,2,256]{3,2,1,0:T(2,128)(2,1)} %pad_maximum_fusion.first.second, bf16[4,128,2,256]{3,2,1,0:T(2,128)(2,1)} %pad_maximum_fusion.first.second, bf16[128,2,256]{2,1,0:T(2,128)(2,1)} %broadcast_in_dim.89.zero), custom_call_target="tpu_custom_call" | custom-call | tf_op jit(solution)/shard_map/pick/pallas_call | solution.py:121
  101.2 6.4 %all-to-all-start.4 = ((bf16[8,128,2,256]{3,2,1,0:T(2,128)(2,1)}), bf16[8,128,2,256]{3,2,1,0:T(2,128)(2,1)S(1)}, u32[]{:S(2)}, u32[]{:S(2)}) async-start(bf16[8,128,2,256]{3,2,1,0:T(2,128)(2,1)} %pick.7), calls=%async_computation.4 | async-start | bytes 2097152 | tf_op jit(solution)/shard_map/all_to_all | solution.py:239
  108.0 1.5 collective-permute-start.17
  109.6 10.5 %collective-permute-done.14.first.second = bf16[4,128,2,256]{3,2,1,0:T(2,128)(2,1)S(1)} collective-permute-done((bf16[4,128,2,256]{3,2,1,0:T(2,128)(2,1)S(1)}, bf16[4,128,2,256]{3,2,1,0:T(2,128)(2,1)S(1)}, u32[]{:S(2)}, u32[]{:S(2)}) %collective-permute-start.14) | collective-permute-done | bytes 524320 | tf_op jit(solution)/shard_map/ppermute | solution.py:231
  121.0 2.2 %pick.6 = bf16[8,128,2,256]{3,2,1,0:T(2,128)(2,1)} custom-call(s32[8]{0:T(128)} %get-tuple-element.11.code, bf16[4,128,2,256]{3,2,1,0:T(2,128)(2,1)} %copy-done.12, bf16[4,128,2,256]{3,2,1,0:T(2,128)(2,1)} %copy-done.12, bf16[128,2,256]{2,1,0:T(2,128)(2,1)} %broadcast_in_dim.89.zero), custom_call_target="tpu_custom_call" | custom-call | tf_op jit(solution)/shard_map/pick/pallas_call | solution.py:121
  124.2 4.5 %all-to-all-start.3 = ((bf16[8,128,2,256]{3,2,1,0:T(2,128)(2,1)}), bf16[8,128,2,256]{3,2,1,0:T(2,128)(2,1)S(1)}, u32[]{:S(2)}, u32[]{:S(2)}) async-start(bf16[8,128,2,256]{3,2,1,0:T(2,128)(2,1)} %pick.6), calls=%async_computation.3 | async-start | bytes 2097152 | tf_op jit(solution)/shard_map/all_to_all | solution.py:239
  128.7 1.4 collective-permute-start.15
  130.1 1.3 collective-permute-start.18
  131.5 2.1 %reshape.303 = bf16[2048,2,128]{2,1,0:T(2,128)(2,1)} reshape(bf16[16,128,256]{2,1,0:T(8,128)(2,1)} %get-tuple-element.6) | data formatting | bytes 2097152 | tf_op jit(solution)/shard_map/reshape;squeeze | solution.py:251
  135.4 1.7 fusion.29
  137.1 5.9 %collective-permute-done.18.second = bf16[4,128,2,256]{3,2,1,0:T(2,128)(2,1)S(1)} collective-permute-done((bf16[4,128,2,256]{3,2,1,0:T(2,128)(2,1)}, bf16[4,128,2,256]{3,2,1,0:T(2,128)(2,1)S(1)}, u32[]{:S(2)}, u32[]{:S(2)}) %collective-permute-start.18) | collective-permute-done | bytes 524320 | tf_op jit(solution)/shard_map/ppermute | solution.py:234
  143.8 2.2 %pick.5 = bf16[8,128,2,256]{3,2,1,0:T(2,128)(2,1)} custom-call(s32[8]{0:T(128)} %get-tuple-element.12.code, bf16[4,128,2,256]{3,2,1,0:T(2,128)(2,1)} %collective-permute-done.17.first, bf16[4,128,2,256]{3,2,1,0:T(2,128)(2,1)} %copy-done.13, bf16[128,2,256]{2,1,0:T(2,128)(2,1)} %broadcast_in_dim.89.zero), custom_call_target="tpu_custom_call" | custom-call | tf_op jit(solution)/shard_map/pick/pallas_call | solution.py:121
  146.1 4.5 %all-to-all-start.2 = ((bf16[8,128,2,256]{3,2,1,0:T(2,128)(2,1)}), bf16[8,128,2,256]{3,2,1,0:T(2,128)(2,1)S(1)}, u32[]{:S(2)}, u32[]{:S(2)}) async-start(bf16[8,128,2,256]{3,2,1,0:T(2,128)(2,1)} %pick.5), calls=%async_computation.2 | async-start | bytes 2097152 | tf_op jit(solution)/shard_map/all_to_all | solution.py:239
  150.6 1.5 convolution_bitcast_fusion.1
  152.1 1.3 collective-permute-start.16
  155.1 8.5 %collective-permute-done.16.second = bf16[4,128,2,256]{3,2,1,0:T(2,128)(2,1)S(1)} collective-permute-done((bf16[4,128,2,256]{3,2,1,0:T(2,128)(2,1)}, bf16[4,128,2,256]{3,2,1,0:T(2,128)(2,1)S(1)}, u32[]{:S(2)}, u32[]{:S(2)}) %collective-permute-start.16) | collective-permute-done | bytes 524320 | tf_op jit(solution)/shard_map/ppermute | solution.py:235
  164.4 2.2 %pick.4 = bf16[8,128,2,256]{3,2,1,0:T(2,128)(2,1)} custom-call(s32[8]{0:T(128)} %get-tuple-element.13.code, bf16[4,128,2,256]{3,2,1,0:T(2,128)(2,1)} %collective-permute-done.15.first, bf16[4,128,2,256]{3,2,1,0:T(2,128)(2,1)} %copy-done.14, bf16[128,2,256]{2,1,0:T(2,128)(2,1)} %broadcast_in_dim.89.zero), custom_call_target="tpu_custom_call" | custom-call | tf_op jit(solution)/shard_map/pick/pallas_call | solution.py:121
  166.7 4.6 %all-to-all-start.1 = ((bf16[8,128,2,256]{3,2,1,0:T(2,128)(2,1)}), bf16[8,128,2,256]{3,2,1,0:T(2,128)(2,1)}, u32[]{:S(2)}, u32[]{:S(2)}) async-start(bf16[8,128,2,256]{3,2,1,0:T(2,128)(2,1)} %pick.4), calls=%async_computation.1 | async-start | bytes 2097152 | tf_op jit(solution)/shard_map/all_to_all | solution.py:239
  171.3 2.0 collective-permute-start.19
  173.4 7.6 %collective-permute-done.19 = f32[32,128]{1,0:T(8,128)S(1)} collective-permute-done((f32[32,128]{1,0:T(8,128)S(1)}, f32[32,128]{1,0:T(8,128)S(1)}, u32[]{:S(2)}, u32[]{:S(2)}) %collective-permute-start.19) | collective-permute-done | bytes 16416 | tf_op jit(solution)/shard_map/ppermute | solution.py:264
  181.1 2.7 %collective-permute-start.20 = (f32[32,128]{1,0:T(8,128)S(1)}, f32[32,128]{1,0:T(8,128)S(1)}, u32[]{:S(2)}, u32[]{:S(2)}) collective-permute-start(f32[32,128]{1,0:T(8,128)S(1)} %fusion.26), channel_id=1, source_target_pairs={{0,8},{4,12},{8,0},{12,4},{1,9},{5,13},{9,1},{13,5},{2,10},{6,14},... | collective-permute-start | bytes 49160 | tf_op jit(solution)/shard_map/ppermute | solution.py:264
  183.8 2.6 %collective-permute-done.20 = f32[32,128]{1,0:T(8,128)S(1)} collective-permute-done((f32[32,128]{1,0:T(8,128)S(1)}, f32[32,128]{1,0:T(8,128)S(1)}, u32[]{:S(2)}, u32[]{:S(2)}) %collective-permute-start.20) | collective-permute-done | bytes 16416 | tf_op jit(solution)/shard_map/ppermute | solution.py:264
  186.4 3.7 %collective-permute-done.21 = f32[32,128]{1,0:T(8,128)S(1)} collective-permute-done((f32[32,128]{1,0:T(8,128)S(1)}, f32[32,128]{1,0:T(8,128)S(1)}, u32[]{:S(2)}, u32[]{:S(2)}) %collective-permute-start.21) | collective-permute-done | bytes 16416 | tf_op jit(solution)/shard_map/ppermute | solution.py:264
  191.2 3.5 %collective-permute-done.22 = f32[32,128]{1,0:T(8,128)S(1)} collective-permute-done((f32[32,128]{1,0:T(8,128)S(1)}, f32[32,128]{1,0:T(8,128)S(1)}, u32[]{:S(2)}, u32[]{:S(2)}) %collective-permute-start.22) | collective-permute-done | bytes 16416 | tf_op jit(solution)/shard_map/ppermute | solution.py:264
  195.3 2.9 %place.4.refs_0_ = bf16[32,128,2,256]{3,2,1,0:T(2,128)(2,1)} custom-call(s32[1]{0:T(128)} %get-tuple-element.14.where, bf16[8,128,2,256]{3,2,1,0:T(2,128)(2,1)} %copy-done.9), custom_call_target="tpu_custom_call" | custom-call | tf_op jit(solution)/shard_map/place/pallas_call | solution.py:142
  198.2 2.8 %place.5.refs_0_ = bf16[32,128,2,256]{3,2,1,0:T(2,128)(2,1)} custom-call(s32[1]{0:T(128)} %get-tuple-element.15.where, bf16[8,128,2,256]{3,2,1,0:T(2,128)(2,1)} %copy-done.7, bf16[32,128,2,256]{3,2,1,0:T(2,128)(2,1)} %place.4.refs_0_), custom_call_target="tpu_custom_call", output_to_operand_aliasing={{}: (2, {})} | custom-call | tf_op jit(solution)/shard_map/place/pallas_call | solution.py:142
  201.0 2.9 %place.6.refs_0_ = bf16[32,128,2,256]{3,2,1,0:T(2,128)(2,1)} custom-call(s32[1]{0:T(128)} %get-tuple-element.16.where, bf16[8,128,2,256]{3,2,1,0:T(2,128)(2,1)} %copy-done.8, bf16[32,128,2,256]{3,2,1,0:T(2,128)(2,1)} %place.5.refs_0_), custom_call_target="tpu_custom_call", output_to_operand_aliasing={{}: (2, {})} | custom-call | tf_op jit(solution)/shard_map/place/pallas_call | solution.py:142
  203.9 2.8 %place.7 = bf16[32,128,2,256]{3,2,1,0:T(2,128)(2,1)} custom-call(s32[1]{0:T(128)} %get-tuple-element.17.where, bf16[8,128,2,256]{3,2,1,0:T(2,128)(2,1)} %all-to-all-done.1.got, bf16[32,128,2,256]{3,2,1,0:T(2,128)(2,1)} %place.6.refs_0_), custom_call_target="tpu_custom_call", output_to_operand_aliasing={{}: (2, {})} | custom-call | tf_op jit(solution)/shard_map/place/pallas_call | solution.py:142
  (134 shorter events, 23.1 us)
Async XLA Ops:
  0.6 134.8 %copy-start = (bf16[4,512]{1,0:T(4,128)(2,1)S(1)}, bf16[4,512]{1,0:T(4,128)(2,1)}, u32[]{:S(2)}) copy-start(bf16[4,512]{1,0:T(4,128)(2,1)} %param.21) | copy-start | bytes 12292
  0.6 47.9 %collective-permute-start.5 = (bf16[288,1152]{1,0:T(8,128)(2,1)}, bf16[288,1152]{1,0:T(8,128)(2,1)S(1)}, u32[]{:S(2)}, u32[]{:S(2)}) collective-permute-start(bf16[288,1152]{1,0:T(8,128)(2,1)} %w_own.1), channel_id=1, source_target_pairs={{0,64},{64,0},{1,65},{65,1},{2,66},{66,2},{3,67},{67,3},{4,68},{68... | collective-permute-start | bytes 1990664 | tf_op jit(solution)/shard_map/ppermute | solution.py:169
  1.7 18.8 %collective-permute-start.6 = (bf16[72,1152]{1,0:T(8,128)(2,1)S(1)}, bf16[72,1152]{1,0:T(8,128)(2,1)S(1)}, u32[]{:S(2)}, u32[]{:S(2)}) collective-permute-start(bf16[72,1152]{1,0:T(8,128)(2,1)S(1)} %constant_dynamic-slice_fusion.1), channel_id=1, source_target_pairs={{0,160},{16,176},{32,128},{48,144},{128,32},{144,48},{160,0},{176,... | collective-permute-start | bytes 497672 | tf_op jit(solution)/shard_map/ppermute | solution.py:173
  9.3 17.1 %collective-permute-start = (bf16[512,288]{1,0:T(8,128)(2,1)S(1)}, bf16[512,288]{1,0:T(8,128)(2,1)S(1)}, u32[]{:S(2)}, u32[]{:S(2)}) collective-permute-start(bf16[512,288]{1,0:T(8,128)(2,1)S(1)} %copy.54), channel_id=1, source_target_pairs={{0,64},{64,160},{16,80},{80,176},{32,96},{96,128},{48,112},{112,14... | collective-permute-start | bytes 884744 | tf_op jit(solution)/shard_map/ppermute | solution.py:166
  20.5 7.5 %collective-permute-start.7 = (bf16[72,1152]{1,0:T(8,128)(2,1)S(1)}, bf16[72,1152]{1,0:T(8,128)(2,1)S(1)}, u32[]{:S(2)}, u32[]{:S(2)}) collective-permute-start(bf16[72,1152]{1,0:T(8,128)(2,1)S(1)} %collective-permute-done.6), channel_id=1, source_target_pairs={{0,4},{4,8},{8,12},{12,0},{1,5},{5,9},{9,13},{13,1},{2,6},{6,10},{... | collective-permute-start | bytes 497672 | tf_op jit(solution)/shard_map/ppermute | solution.py:175
  22.0 9.7 %collective-permute-start.8 = (bf16[72,1152]{1,0:T(8,128)(2,1)S(1)}, bf16[72,1152]{1,0:T(8,128)(2,1)S(1)}, u32[]{:S(2)}, u32[]{:S(2)}) collective-permute-start(bf16[72,1152]{1,0:T(8,128)(2,1)S(1)} %collective-permute-done.6), channel_id=1, source_target_pairs={{0,8},{4,12},{8,0},{12,4},{1,9},{5,13},{9,1},{13,5},{2,10},{6,14},... | collective-permute-start | bytes 497672 | tf_op jit(solution)/shard_map/ppermute | solution.py:177
  24.9 6.9 %collective-permute-start.9 = (bf16[72,1152]{1,0:T(8,128)(2,1)S(1)}, bf16[72,1152]{1,0:T(8,128)(2,1)S(1)}, u32[]{:S(2)}, u32[]{:S(2)}) collective-permute-start(bf16[72,1152]{1,0:T(8,128)(2,1)S(1)} %collective-permute-done.6), channel_id=1, source_target_pairs={{0,12},{4,0},{8,4},{12,8},{1,13},{5,1},{9,5},{13,9},{2,14},{6,2},{... | collective-permute-start | bytes 497672 | tf_op jit(solution)/shard_map/ppermute | solution.py:176
  26.4 12.9 %copy-start.3 = (bf16[512,288]{1,0:T(8,128)(2,1)}, bf16[512,288]{1,0:T(8,128)(2,1)S(1)}, u32[]{:S(2)}) copy-start(bf16[512,288]{1,0:T(8,128)(2,1)S(1)} %collective-permute-done.x_own) | copy-start | bytes 884740
  26.4 9.4 %collective-permute-start.1 = (bf16[512,288]{1,0:T(8,128)(2,1)S(1)}, bf16[512,288]{1,0:T(8,128)(2,1)S(1)}, u32[]{:S(2)}, u32[]{:S(2)}) collective-permute-start(bf16[512,288]{1,0:T(8,128)(2,1)S(1)} %collective-permute-done.x_own), channel_id=1, source_target_pairs={{0,1},{1,2},{2,3},{3,0},{4,5},{5,6},{6,7},{7,4},{8,9},{9,10},{10,1... | collective-permute-start | bytes 884744 | tf_op jit(solution)/shard_map/ppermute | solution.py:185
  28.0 10.1 %collective-permute-start.2 = (bf16[512,288]{1,0:T(8,128)(2,1)S(1)}, bf16[512,288]{1,0:T(8,128)(2,1)S(1)}, u32[]{:S(2)}, u32[]{:S(2)}) collective-permute-start(bf16[512,288]{1,0:T(8,128)(2,1)S(1)} %collective-permute-done.x_own), channel_id=1, source_target_pairs={{0,3},{1,0},{2,1},{3,2},{4,7},{5,4},{6,5},{7,6},{8,11},{9,8},{10,9... | collective-permute-start | bytes 884744 | tf_op jit(solution)/shard_map/ppermute | solution.py:186
  31.9 16.7 %collective-permute-start.10 = (bf16[288,1152]{1,0:T(8,128)(2,1)S(1)}, bf16[288,1152]{1,0:T(8,128)(2,1)S(1)}, u32[]{:S(2)}, u32[]{:S(2)}) collective-permute-start(bf16[288,1152]{1,0:T(8,128)(2,1)S(1)} %bitcast.95), channel_id=1, source_target_pairs={{0,64},{64,0},{1,65},{65,1},{2,66},{66,2},{3,67},{67,3},{4,68},{68... | collective-permute-start | bytes 1990664 | tf_op jit(solution)/shard_map/ppermute | solution.py:182
  36.5 10.9 %collective-permute-start.3 = (bf16[256,288]{1,0:T(8,128)(2,1)}, bf16[256,288]{1,0:T(8,128)(2,1)}, u32[]{:S(2)}, u32[]{:S(2)}) collective-permute-start(bf16[256,288]{1,0:T(8,128)(2,1)} %slice.74), channel_id=1, source_target_pairs={{0,1},{1,2},{2,3},{3,0},{4,5},{5,6},{6,7},{7,4},{8,9},{9,10},{10,1... | collective-permute-start | bytes 442376 | tf_op jit(solution)/shard_map/ppermute | solution.py:187
  38.7 8.7 %collective-permute-start.4 = (bf16[256,288]{1,0:T(8,128)(2,1)}, bf16[256,288]{1,0:T(8,128)(2,1)}, u32[]{:S(2)}, u32[]{:S(2)}) collective-permute-start(bf16[256,288]{1,0:T(8,128)(2,1)} %slice.75), channel_id=1, source_target_pairs={{0,3},{1,0},{2,1},{3,2},{4,7},{5,4},{6,5},{7,6},{8,11},{9,8},{10,9... | collective-permute-start | bytes 442376 | tf_op jit(solution)/shard_map/ppermute | solution.py:188
  39.3 6.5 %copy-start.15 = (f32[1152]{0:T(1024)S(1)}, f32[1152]{0:T(1024)}, u32[]{:S(2)}) copy-start(f32[1152]{0:T(1024)} %param.15) | copy-start | bytes 13828
  39.3 6.6 %copy-start.16 = (f32[1152]{0:T(1024)S(1)}, f32[1152]{0:T(1024)}, u32[]{:S(2)}) copy-start(f32[1152]{0:T(1024)} %param.16) | copy-start | bytes 13828
  39.3 6.7 %copy-start.17 = (f32[1152]{0:T(1024)S(1)}, f32[1152]{0:T(1024)}, u32[]{:S(2)}) copy-start(f32[1152]{0:T(1024)} %param.18) | copy-start | bytes 13828
  39.3 6.7 %copy-start.18 = (f32[1152]{0:T(1024)S(1)}, f32[1152]{0:T(1024)}, u32[]{:S(2)}) copy-start(f32[1152]{0:T(1024)} %param.19) | copy-start | bytes 13828
  39.3 9.2 %copy-start.2 = (bf16[288,1152]{1,0:T(8,128)(2,1)S(1)}, bf16[288,1152]{1,0:T(8,128)(2,1)}, u32[]{:S(2)}) copy-start(bf16[288,1152]{1,0:T(8,128)(2,1)} %w_own.1) | copy-start | bytes 1990660
  48.5 2.3 %copy-start.1 = (bf16[144,8,2,1024]{3,1,2,0:T(8,128)(2,1)S(1)}, bf16[144,8,2,1024]{3,1,2,0:T(8,128)(2,1)}, u32[]{:S(2)}) copy-start(bf16[144,8,2,1024]{3,1,2,0:T(8,128)(2,1)} %copy.85) | copy-start | bytes 14155780
  50.9 1.0 copy-start.4
  62.7 8.2 %copy-start.5 = (bf16[16,128,2,256]{3,2,1,0:T(2,128)(2,1)S(1)}, bf16[16,128,2,256]{3,2,1,0:T(2,128)(2,1)}, u32[]{:S(2)}) copy-start(bf16[16,128,2,256]{3,2,1,0:T(2,128)(2,1)} %param.22) | copy-start | bytes 6291460
  62.8 30.5 %all-to-all-start = ((bf16[4,512,512]{2,1,0:T(8,128)(2,1)}), bf16[4,512,512]{2,1,0:T(8,128)(2,1)}, u32[]{:S(2)}, u32[]{:S(2)}) async-start(bf16[4,512,512]{2,1,0:T(8,128)(2,1)} %get-tuple-element.4), calls=%async_computation | async-start | bytes 4194304 | tf_op jit(solution)/shard_map/all_to_all | solution.py:204
  70.3 14.3 %copy-start.19 = (s32[1,4]{1,0:T(1,128)S(1)}, s32[1,4]{1,0:T(1,128)}, u32[]{:S(2)}) copy-start(s32[1,4]{1,0:T(1,128)} %param.23) | copy-start | bytes 52
  80.5 10.9 %collective-permute-start.11 = (f32[8,512]{1,0:T(8,128)S(1)}, f32[8,512]{1,0:T(8,128)S(1)}, u32[]{:S(2)}, u32[]{:S(2)}) collective-permute-start(f32[8,512]{1,0:T(8,128)S(1)} %get-tuple-element.5), channel_id=1, source_target_pairs={{0,1},{1,2},{2,3},{3,0},{4,5},{5,6},{6,7},{7,4},{8,9},{9,10},{10,1... | collective-permute-start | bytes 49160 | tf_op jit(solution)/shard_map/ppermute | solution.py:202
  81.9 9.4 %collective-permute-start.12 = (f32[8,512]{1,0:T(8,128)S(1)}, f32[8,512]{1,0:T(8,128)S(1)}, u32[]{:S(2)}, u32[]{:S(2)}) collective-permute-start(f32[8,512]{1,0:T(8,128)S(1)} %get-tuple-element.5), channel_id=1, source_target_pairs={{0,3},{1,0},{2,1},{3,2},{4,7},{5,4},{6,5},{7,6},{8,11},{9,8},{10,9... | collective-permute-start | bytes 49160 | tf_op jit(solution)/shard_map/ppermute | solution.py:202
  82.5 10.8 %collective-permute-start.13 = (f32[8,512]{1,0:T(8,128)S(1)}, f32[8,512]{1,0:T(8,128)S(1)}, u32[]{:S(2)}, u32[]{:S(2)}) collective-permute-start(f32[8,512]{1,0:T(8,128)S(1)} %get-tuple-element.5), channel_id=1, source_target_pairs={{0,2},{1,3},{2,0},{3,1},{4,6},{5,7},{6,4},{7,5},{8,10},{9,11},{10,... | collective-permute-start | bytes 49160 | tf_op jit(solution)/shard_map/ppermute | solution.py:202
  95.4 14.0 %copy-start.20 = (s32[1,16]{1,0:T(1,128)S(1)}, s32[1,16]{1,0:T(1,128)}, u32[]{:S(2)}) copy-start(s32[1,16]{1,0:T(1,128)} %param.24) | copy-start | bytes 196
  95.5 0.8 copy-start.10
  98.2 9.4 %copy-start.6 = (bf16[4,128,2,256]{3,2,1,0:T(2,128)(2,1)S(1)}, bf16[4,128,2,256]{3,2,1,0:T(2,128)(2,1)}, u32[]{:S(2)}) copy-start(bf16[4,128,2,256]{3,2,1,0:T(2,128)(2,1)} %pad_maximum_fusion.first.second) | copy-start | bytes 1572868
  101.2 21.9 %all-to-all-start.4 = ((bf16[8,128,2,256]{3,2,1,0:T(2,128)(2,1)}), bf16[8,128,2,256]{3,2,1,0:T(2,128)(2,1)S(1)}, u32[]{:S(2)}, u32[]{:S(2)}) async-start(bf16[8,128,2,256]{3,2,1,0:T(2,128)(2,1)} %pick.7), calls=%async_computation.4 | async-start | bytes 2097152 | tf_op jit(solution)/shard_map/all_to_all | solution.py:239
  107.6 12.5 %collective-permute-start.14 = (bf16[4,128,2,256]{3,2,1,0:T(2,128)(2,1)S(1)}, bf16[4,128,2,256]{3,2,1,0:T(2,128)(2,1)S(1)}, u32[]{:S(2)}, u32[]{:S(2)}) collective-permute-start(bf16[4,128,2,256]{3,2,1,0:T(2,128)(2,1)S(1)} %copy-done.6), channel_id=1, source_target_pairs={{0,16},{16,0},{32,48},{48,32},{1,17},{17,1},{33,49},{49,33},{2,18}... | collective-permute-start | bytes 1572872 | tf_op jit(solution)/shard_map/ppermute | solution.py:231
  108.0 22.2 %collective-permute-start.17 = (bf16[4,128,2,256]{3,2,1,0:T(2,128)(2,1)S(1)}, bf16[4,128,2,256]{3,2,1,0:T(2,128)(2,1)}, u32[]{:S(2)}, u32[]{:S(2)}) collective-permute-start(bf16[4,128,2,256]{3,2,1,0:T(2,128)(2,1)S(1)} %copy-done.6), channel_id=1, source_target_pairs={{16,32},{32,16},{17,33},{33,17},{18,34},{34,18},{19,35},{35,19},{2... | collective-permute-start | bytes 1572872 | tf_op jit(solution)/shard_map/ppermute | solution.py:232
  120.1 0.8 copy-start.12
  121.0 13.8 %copy-start.21 = (s32[1,2]{1,0:T(1,128)S(1)}, s32[1,2]{1,0:T(1,128)}, u32[]{:S(2)}) copy-start(s32[1,2]{1,0:T(1,128)} %param.26) | copy-start | bytes 28
  123.2 1.0 copy-start.9
  124.2 21.9 %all-to-all-start.3 = ((bf16[8,128,2,256]{3,2,1,0:T(2,128)(2,1)}), bf16[8,128,2,256]{3,2,1,0:T(2,128)(2,1)S(1)}, u32[]{:S(2)}, u32[]{:S(2)}) async-start(bf16[8,128,2,256]{3,2,1,0:T(2,128)(2,1)} %pick.6), calls=%async_computation.3 | async-start | bytes 2097152 | tf_op jit(solution)/shard_map/all_to_all | solution.py:239
  128.7 23.4 %collective-permute-start.15 = (bf16[4,128,2,256]{3,2,1,0:T(2,128)(2,1)}, bf16[4,128,2,256]{3,2,1,0:T(2,128)(2,1)}, u32[]{:S(2)}, u32[]{:S(2)}) collective-permute-start(bf16[4,128,2,256]{3,2,1,0:T(2,128)(2,1)} %copy-done.12), channel_id=1, source_target_pairs={{16,32},{32,16},{17,33},{33,17},{18,34},{34,18},{19,35},{35,19},{2... | collective-permute-start | bytes 1572872 | tf_op jit(solution)/shard_map/ppermute | solution.py:233
  130.1 12.9 %collective-permute-start.18 = (bf16[4,128,2,256]{3,2,1,0:T(2,128)(2,1)}, bf16[4,128,2,256]{3,2,1,0:T(2,128)(2,1)S(1)}, u32[]{:S(2)}, u32[]{:S(2)}) collective-permute-start(bf16[4,128,2,256]{3,2,1,0:T(2,128)(2,1)} %collective-permute-done.17.first), channel_id=1, source_target_pairs={{16,0},{32,48},{17,1},{33,49},{18,2},{34,50},{19,3},{35,51},{20,4}... | collective-permute-start | bytes 1572872 | tf_op jit(solution)/shard_map/ppermute | solution.py:234
  133.6 20.4 %copy-start.11 = (bf16[512,256]{1,0:T(8,128)(2,1)S(1)}, bf16[512,256]{1,0:T(8,128)(2,1)}, u32[]{:S(2)}) copy-start(bf16[512,256]{1,0:T(8,128)(2,1)} %copy-done.10) | copy-start | bytes 786436
  146.0 20.6 %copy-start.7 = (bf16[8,128,2,256]{3,2,1,0:T(2,128)(2,1)}, bf16[8,128,2,256]{3,2,1,0:T(2,128)(2,1)S(1)}, u32[]{:S(2)}) copy-start(bf16[8,128,2,256]{3,2,1,0:T(2,128)(2,1)S(1)} %all-to-all-done.3.got) | copy-start | bytes 3145732
  146.1 20.6 %all-to-all-start.2 = ((bf16[8,128,2,256]{3,2,1,0:T(2,128)(2,1)}), bf16[8,128,2,256]{3,2,1,0:T(2,128)(2,1)S(1)}, u32[]{:S(2)}, u32[]{:S(2)}) async-start(bf16[8,128,2,256]{3,2,1,0:T(2,128)(2,1)} %pick.5), calls=%async_computation.2 | async-start | bytes 2097152 | tf_op jit(solution)/shard_map/all_to_all | solution.py:239
  152.1 11.5 %collective-permute-start.16 = (bf16[4,128,2,256]{3,2,1,0:T(2,128)(2,1)}, bf16[4,128,2,256]{3,2,1,0:T(2,128)(2,1)S(1)}, u32[]{:S(2)}, u32[]{:S(2)}) collective-permute-start(bf16[4,128,2,256]{3,2,1,0:T(2,128)(2,1)} %collective-permute-done.15.first), channel_id=1, source_target_pairs={{16,0},{32,48},{17,1},{33,49},{18,2},{34,50},{19,3},{35,51},{20,4}... | collective-permute-start | bytes 1572872 | tf_op jit(solution)/shard_map/ppermute | solution.py:235
  166.6 34.4 %copy-start.8 = (bf16[8,128,2,256]{3,2,1,0:T(2,128)(2,1)}, bf16[8,128,2,256]{3,2,1,0:T(2,128)(2,1)S(1)}, u32[]{:S(2)}) copy-start(bf16[8,128,2,256]{3,2,1,0:T(2,128)(2,1)S(1)} %all-to-all-done.2.got) | copy-start | bytes 3145732
  166.7 37.3 %all-to-all-start.1 = ((bf16[8,128,2,256]{3,2,1,0:T(2,128)(2,1)}), bf16[8,128,2,256]{3,2,1,0:T(2,128)(2,1)}, u32[]{:S(2)}, u32[]{:S(2)}) async-start(bf16[8,128,2,256]{3,2,1,0:T(2,128)(2,1)} %pick.4), calls=%async_computation.1 | async-start | bytes 2097152 | tf_op jit(solution)/shard_map/all_to_all | solution.py:239
  171.3 9.7 %collective-permute-start.19 = (f32[32,128]{1,0:T(8,128)S(1)}, f32[32,128]{1,0:T(8,128)S(1)}, u32[]{:S(2)}, u32[]{:S(2)}) collective-permute-start(f32[32,128]{1,0:T(8,128)S(1)} %pad_maximum_fusion.2), channel_id=1, source_target_pairs={{0,4},{4,0},{8,12},{12,8},{1,5},{5,1},{9,13},{13,9},{2,6},{6,2},{1... | collective-permute-start | bytes 49160 | tf_op jit(solution)/shard_map/ppermute | solution.py:264
  181.1 5.2 %collective-permute-start.20 = (f32[32,128]{1,0:T(8,128)S(1)}, f32[32,128]{1,0:T(8,128)S(1)}, u32[]{:S(2)}, u32[]{:S(2)}) collective-permute-start(f32[32,128]{1,0:T(8,128)S(1)} %fusion.26), channel_id=1, source_target_pairs={{0,8},{4,12},{8,0},{12,4},{1,9},{5,13},{9,1},{13,5},{2,10},{6,14},... | collective-permute-start | bytes 49160 | tf_op jit(solution)/shard_map/ppermute | solution.py:264
  186.3 3.7 %collective-permute-start.21 = (f32[32,128]{1,0:T(8,128)S(1)}, f32[32,128]{1,0:T(8,128)S(1)}, u32[]{:S(2)}, u32[]{:S(2)}) collective-permute-start(f32[32,128]{1,0:T(8,128)S(1)} %add.231), channel_id=1, source_target_pairs={{0,16},{16,0},{32,48},{48,32},{1,17},{17,1},{33,49},{49,33},{2,18}... | collective-permute-start | bytes 49160 | tf_op jit(solution)/shard_map/ppermute | solution.py:264
  190.1 4.6 %collective-permute-start.22 = (f32[32,128]{1,0:T(8,128)S(1)}, f32[32,128]{1,0:T(8,128)S(1)}, u32[]{:S(2)}, u32[]{:S(2)}) collective-permute-start(f32[32,128]{1,0:T(8,128)S(1)} %add.232), channel_id=1, source_target_pairs={{0,32},{16,48},{32,0},{48,16},{1,33},{17,49},{33,1},{49,17},{2,34}... | collective-permute-start | bytes 49160 | tf_op jit(solution)/shard_map/ppermute | solution.py:264
  (2 other events, 1.6 us)
